TPU v7x, 128 devices: a whole 4x4x4 slice. The times are simulated.
128 devices in a mesh: dp: 4 (over x), space: 32 (over y, z, core).
Axes of the slice: x: 4, y: 4, z: 4, core: 2. Of those that a mesh axis runs over, the one named last changes fastest.
Arguments:
- fields: bfloat16 [4, 256, 64, 4096], P('dp', 'space'), may hold values from -6 to 6
- cotangent: bfloat16 [4, 256, 64, 4096], P('dp', 'space'), may hold values from -6 to 6
- mode_weight: bfloat16 [128, 64, 64, 128], P('space'), may hold values from -4 to 4
- mix_weight: bfloat16 [64, 64], replicated, may hold values from -0.75 to 0.75
Outputs:
- response: bfloat16 [4, 256, 64, 4096], P('dp', 'space')
- field_grad: bfloat16 [4, 256, 64, 4096], P('dp', 'space')
- mode_grad: float32 [128, 64, 64, 128], P('space', 'dp')
All inputs are finite; a program needn't handle non-finite values.
Results may differ from a plain program's by a relative error of at most 0.035.
Values may be sent and summed in bfloat16 or wider, within the bound.
No kernel may reach another device: no remote copies, remote signals or barrier semaphores. Data moves between devices by JAX's collectives and lax.ppermute only.
A program may use at most 128 MiB of HBM per device.

v0:
```python
import math

import jax
import jax.numpy as jnp
from jax import lax
from jax.sharding import PartitionSpec as P

GELU_CUBIC = 0.044715
GELU_SCALE = math.sqrt(2.0 / math.pi)


def gelu_value(values):
    inner_arg = GELU_SCALE * (values + GELU_CUBIC * values * values * values)
    return 0.5 * values * (1.0 + jnp.tanh(inner_arg))


def gelu_slope(values):
    tangent = jnp.tanh(GELU_SCALE * (values + GELU_CUBIC * values * values * values))
    return 0.5 * (1.0 + tangent) + 0.5 * values * (1.0 - tangent * tangent) * GELU_SCALE * (
        1.0 + 3.0 * GELU_CUBIC * values * values
    )


def column_angles(length, mode_count):
    positions = lax.iota(jnp.int32, length)
    frequencies = lax.iota(jnp.int32, mode_count)
    phase_index = positions[:, None] * frequencies[None, :] % length
    return phase_index.astype(jnp.float32) * (2.0 * math.pi / length)


def column_factor(mode_count):
    frequencies = lax.iota(jnp.int32, mode_count)
    single = jnp.where(frequencies == 0, 1.0, 2.0).astype(jnp.bfloat16)
    return jnp.concatenate([single, single], axis=0)


def forward_table(length, mode_count, weighted):
    angles = column_angles(length, mode_count)
    norm_scale = 1.0 / math.sqrt(length)
    table_out = jnp.concatenate(
        [jnp.cos(angles) * norm_scale, -jnp.sin(angles) * norm_scale], axis=1
    ).astype(jnp.bfloat16)
    if weighted:
        table_out = table_out * column_factor(mode_count)[None, :]
    return table_out


def inverse_table(length, mode_count, weighted):
    angles = column_angles(length, mode_count).T
    norm_scale = 1.0 / math.sqrt(length)
    table_out = jnp.concatenate(
        [jnp.cos(angles) * norm_scale, -jnp.sin(angles) * norm_scale], axis=0
    ).astype(jnp.bfloat16)
    if weighted:
        table_out = table_out * column_factor(mode_count)[:, None]
    return table_out


def row_tables(extent, mode_count, offset, length):
    slot_index = lax.iota(jnp.int32, mode_count)
    frequencies = jnp.where(
        slot_index < mode_count // 2, slot_index, extent - mode_count + slot_index
    )
    rows_here = offset + lax.iota(jnp.int32, length)
    phase_index = frequencies[:, None] * rows_here[None, :] % extent
    angles = phase_index.astype(jnp.float32) * (2.0 * math.pi / extent)
    norm_scale = 1.0 / math.sqrt(extent)
    return (
        (jnp.cos(angles) * norm_scale).astype(jnp.bfloat16),
        (jnp.sin(angles) * norm_scale).astype(jnp.bfloat16),
    )


def row_forward(cos_table, sin_table, columns):
    cos_part = jnp.einsum("kr,rcpy->ykpc", cos_table, columns, preferred_element_type=jnp.float32)
    sin_part = jnp.einsum("kr,rcpy->ykpc", sin_table, columns, preferred_element_type=jnp.float32)
    real_part = cos_part[:, :, 0] + sin_part[:, :, 1]
    imag_part = cos_part[:, :, 1] - sin_part[:, :, 0]
    return jnp.concatenate([real_part, imag_part], axis=-1)


def row_inverse(cos_table, sin_table, spectrum):
    channels = spectrum.shape[2] // 2
    cos_part = jnp.einsum("kr,ykd->rdy", cos_table, spectrum, preferred_element_type=jnp.float32)
    sin_part = jnp.einsum("kr,ykd->rdy", sin_table, spectrum, preferred_element_type=jnp.float32)
    real_part = cos_part[:, :channels] - sin_part[:, channels:]
    imag_part = cos_part[:, channels:] + sin_part[:, :channels]
    return jnp.stack([real_part, imag_part], axis=2)


def mix_modes(spectrum, weight):
    channels = weight.shape[2]
    real_prod = jnp.einsum(
        "ykc,ykcd->ykd", spectrum[..., :channels], weight, preferred_element_type=jnp.float32
    )
    imag_prod = jnp.einsum(
        "ykc,ykcd->ykd", spectrum[..., channels:], weight, preferred_element_type=jnp.float32
    )
    return jnp.concatenate(
        [
            real_prod[..., :channels] - imag_prod[..., channels:],
            real_prod[..., channels:] + imag_prod[..., :channels],
        ],
        axis=-1,
    )


def mix_adjoint(delta_modes, weight):
    channels = weight.shape[2]
    swapped = jnp.concatenate([delta_modes[..., channels:], -delta_modes[..., :channels]], axis=-1)
    first_half = jnp.einsum(
        "ykd,ykcd->ykc", delta_modes, weight, preferred_element_type=jnp.float32
    )
    second_half = jnp.einsum("ykd,ykcd->ykc", swapped, weight, preferred_element_type=jnp.float32)
    return jnp.concatenate([first_half, second_half], axis=-1)


def weight_grad(spectrum, delta_modes):
    channels = spectrum.shape[2] // 2
    swapped = jnp.concatenate([delta_modes[..., channels:], -delta_modes[..., :channels]], axis=-1)
    real_term = jnp.einsum(
        "ykc,ykd->ykcd", spectrum[..., :channels], delta_modes, preferred_element_type=jnp.float32
    )
    imag_term = jnp.einsum(
        "ykc,ykd->ykcd", spectrum[..., channels:], swapped, preferred_element_type=jnp.float32
    )
    return real_term + imag_term


def on_device(fields, cotangent, mode_weight, mix_weight):
    signal = fields[0]
    upstream = cotangent[0]
    rows_here, channels, length = signal.shape
    mode_rows = mode_weight.shape[0]
    kx_count = mode_weight.shape[1]
    groups = lax.axis_size("space")
    ky_count = mode_rows * groups
    extent = rows_here * groups
    forward_cols = forward_table(length, ky_count, False)
    weighted_cols = forward_table(length, ky_count, True)
    inverse_cols = inverse_table(length, ky_count, True)
    plain_inverse = inverse_table(length, ky_count, False)
    offset = lax.axis_index("space") * rows_here
    local_cos, local_sin = row_tables(extent, kx_count, offset, rows_here)

    def to_modes(columns):
        return lax.psum_scatter(
            row_forward(local_cos, local_sin, columns).astype(jnp.bfloat16),
            "space",
            scatter_dimension=0,
            tiled=True,
        )

    def to_rows(spectrum):
        return row_inverse(
            local_cos, local_sin, lax.all_gather(spectrum, "space", axis=0, tiled=True)
        ).astype(jnp.bfloat16)

    columns = jnp.dot(
        signal.reshape(rows_here * channels, length),
        forward_cols,
        preferred_element_type=jnp.float32,
    )
    columns = columns.astype(jnp.bfloat16).reshape(rows_here, channels, 2, ky_count)
    spectrum = to_modes(columns)
    modes_out = mix_modes(spectrum, mode_weight).astype(jnp.bfloat16)
    back_columns = to_rows(modes_out)
    spectral = jnp.dot(
        back_columns.reshape(rows_here * channels, 2 * ky_count),
        inverse_cols,
        preferred_element_type=jnp.float32,
    )
    spectral = spectral.reshape(rows_here, channels, length)
    preact = spectral + jnp.einsum(
        "rcn,cd->rdn", signal, mix_weight, preferred_element_type=jnp.float32
    )
    response = gelu_value(preact).astype(jnp.bfloat16)
    delta_field = (upstream.astype(jnp.float32) * gelu_slope(preact)).astype(jnp.bfloat16)
    delta_cols = jnp.dot(
        delta_field.reshape(rows_here * channels, length),
        weighted_cols,
        preferred_element_type=jnp.float32,
    )
    delta_cols = delta_cols.astype(jnp.bfloat16).reshape(rows_here, channels, 2, ky_count)
    delta_modes = to_modes(delta_cols)
    input_modes = mix_adjoint(delta_modes, mode_weight).astype(jnp.bfloat16)
    grad_local = weight_grad(spectrum, delta_modes)
    mode_grad = lax.psum_scatter(
        grad_local.astype(jnp.bfloat16), "dp", scatter_dimension=1, tiled=True
    ).astype(jnp.float32)
    input_cols = to_rows(input_modes)
    field_grad = jnp.dot(
        input_cols.reshape(rows_here * channels, 2 * ky_count),
        plain_inverse,
        preferred_element_type=jnp.float32,
    )
    field_grad = field_grad.reshape(rows_here, channels, length)
    field_grad = field_grad + jnp.einsum(
        "rdn,cd->rcn", delta_field, mix_weight, preferred_element_type=jnp.float32
    )
    return (response[None], field_grad.astype(jnp.bfloat16)[None], mode_grad)


def solution(mesh):
    in_specs = (
        P("dp", "space", None, None),
        P("dp", "space", None, None),
        P("space", None, None, None),
        P(),
    )
    out_specs = (
        P("dp", "space", None, None),
        P("dp", "space", None, None),
        P("space", "dp", None, None),
    )
    return jax.shard_map(
        on_device, mesh=mesh, in_specs=in_specs, out_specs=out_specs, check_vma=False
    )
```

profile of v0, /device:TPU:1, one launch (start us, length us, event | category | flops | bytes accessed | tf_op | source)
XLA Modules:
  0.0 377.6 jit_solution(5238253479102441029)
XLA Ops:
  7.2 8.6 %multiply_convert_fusion.3 = (bf16[4096,128]{1,0:T(8,128)(2,1)S(1)}, bf16[4096,128]{1,0:T(8,128)(2,1)S(1)}) fusion(), kind=kLoop, calls=%fused_computation.61 | loop fusion | flops 9961472 | bytes 2097152 | tf_op jit(solution)/shard_map/convert.28
  15.9 3.9 %fusion.41 = bf16[512,256]{0,1:T(8,128)(2,1)S(1)} fusion(bf16[512,4096]{1,0:T(8,128)(2,1)} %bitcast.175, bf16[4096,128]{1,0:T(8,128)(2,1)S(1)} %get-tuple-element.19, bf16[4096,128]{1,0:T(8,128)(2,1)S(1)} %get-tuple-element.20), kind=kOutput, calls=%fused_computation.74 | convolution fusion | flops 1078067200 | bytes 6553600 | tf_op jit(solution)/shard_map/dot_general | solution.py:159
  22.9 3.3 copy.48
  26.2 80.8 %reduce-scatter.7.cloned.1.call-done = bf16[4,64,128]{2,1,0:T(8,128)(2,1)} async-done(((bf16[128,64,128]{2,1,0:T(8,128)(2,1)}), bf16[4,64,128]{2,1,0:T(8,128)(2,1)}) %reduce-scatter.7.cloned.1.call-update) | async-done | bytes 65552 | tf_op jit(solution)/shard_map/reduce_scatter | solution.py:147
  108.1 3.6 fusion.68
  114.0 8.5 %multiply_convert_fusion.1 = (bf16[128,4096]{1,0:T(8,128)(2,1)S(1)}, bf16[128,4096]{1,0:T(8,128)(2,1)S(1)}) fusion(), kind=kLoop, calls=%fused_computation.57 | loop fusion | flops 9961472 | bytes 2097152 | tf_op jit(solution)/shard_map/convert.16
  122.6 36.6 %all-gather.3.cloned.1.call-done = bf16[128,64,128]{2,1,0:T(8,128)(2,1)} async-done(((bf16[4,64,128]{2,1,0:T(8,128)(2,1)}), bf16[128,64,128]{2,1,0:T(8,128)(2,1)}) %all-gather.3.cloned.1.call-update) | async-done | bytes 2097168 | tf_op jit(solution)/shard_map/all_gather | solution.py:156
  159.2 2.1 convolution_bitcast_fusion.6
  161.3 2.1 convolution_bitcast_fusion.7
  167.3 8.5 %fusion.6 = (bf16[8,64,4096]{2,1,0:T(8,128)(2,1)S(1)}, bf16[1,8,64,4096]{3,2,1,0:T(8,128)(2,1)}) fusion(bf16[1,8,64,4096]{3,2,1,0:T(8,128)(2,1)S(1)} %copy-done.6, f32[8,64,4096]{2,1,0:T(8,128)S(1)} %fusion.25, bf16[1,8,64,4096]{3,2,1,0:T(8,128)(2,1)S(1)} %copy-done.7, bf16[64,64]{1,0:T(8,128)(2,1)S(1)} %copy-done), kind=kOutput, calls=%fused_computation.8 | convolution fusion | flops 316669952 | bytes 25174016 | tf_op jit(solution)/shard_map/rcn,cd->rdn/dot_general | solution.py:174
  175.8 2.0 copy-done.1
  177.8 2.0 fusion.38
  185.0 4.6 %copy.56 = bf16[128,64,128]{2,1,0:T(8,128)(2,1)} copy(bf16[128,64,128]{0,1,2:T(8,128)(2,1)} %pad_maximum_fusion.3) | data formatting | bytes 4194304 | tf_op jit(solution)/shard_map/concatenate | solution.py:79
  189.8 76.1 %reduce-scatter.9.cloned.1.call-done = bf16[4,64,128]{2,1,0:T(8,128)(2,1)} async-done(((bf16[128,64,128]{2,1,0:T(8,128)(2,1)}), bf16[4,64,128]{2,1,0:T(8,128)(2,1)}) %reduce-scatter.9.cloned.1.call-update) | async-done | bytes 65552 | tf_op jit(solution)/shard_map/reduce_scatter | solution.py:147
  267.2 4.6 %fusion.64 = f32[4,64,1,64]{3,2,1,0:T(1,128)S(1)} fusion(bf16[4,64,64,128]{3,2,1,0:T(8,128)(2,1)} %param.6, bf16[4,64,128,1]{2,1,0,3:T(8,128)(2,1)S(1)} %get-tuple-element.12), kind=kOutput, calls=%fused_computation.106 | convolution fusion | flops 4194304 | bytes 4325376 | tf_op jit(solution)/shard_map/ykd,ykcd->ykc/dot_general | solution.py:114
  271.8 2.3 fusion.66
  275.0 5.4 %add_convert_fusion = bf16[4,64,64,128]{3,2,1,0:T(8,128)(2,1)S(1)} fusion(f32[4,64,128]{2,1,0:T(8,128)S(1)} %get-tuple-element.11, f32[4,64,64]{2,1,0:T(8,128)S(1)} %get-tuple-element.14, f32[4,64,128]{2,1,0:T(8,128)S(1)} %convert.86, f32[4,64,64]{2,1,0:T(8,128)S(1)} %get-tuple-element.13), kind=kLoop, calls=%fused_computation.12 | loop fusion | flops 8388608 | bytes 4587520 | tf_op jit(solution)/shard_map/convert_element_type | solution.py:189
  281.8 4.8 %copy.103 = bf16[8,8,256,128]{3,1,2,0:T(8,128)(2,1)} copy(bf16[8,8,256,128]{3,2,1,0:T(8,128)(2,1)S(1)} %bitcast.164) | data formatting | bytes 8388608
  286.6 33.6 %all-gather.5.cloned.1.call-done = bf16[128,64,128]{2,1,0:T(8,128)(2,1)} async-done(((bf16[4,64,128]{2,1,0:T(8,128)(2,1)}), bf16[128,64,128]{2,1,0:T(8,128)(2,1)}) %all-gather.5.cloned.1.call-update) | async-done | bytes 2097168 | tf_op jit(solution)/shard_map/all_gather | solution.py:156
  320.2 2.1 convolution_bitcast_fusion.4
  322.3 2.1 convolution_bitcast_fusion.5
  327.1 3.3 fusion.8
  330.3 37.8 %reduce-scatter.11.cloned.1.call-done = bf16[16,32768]{1,0:T(8,128)(2,1)} async-done(((bf16[64,32768]{1,0:T(8,128)(2,1)}), bf16[16,32768]{1,0:T(8,128)(2,1)}) %reduce-scatter.11.cloned.1.call-update) | async-done | bytes 1048592
  369.5 1.6 copy_convert_fusion
  (64 shorter events, 23.5 us)
Async XLA Ops:
  7.2 158.1 %copy-start = (bf16[64,64]{1,0:T(8,128)(2,1)S(1)}, bf16[64,64]{1,0:T(8,128)(2,1)}, u32[]{:S(2)}) copy-start(bf16[64,64]{1,0:T(8,128)(2,1)} %param.7) | copy-start | bytes 24580
  7.2 99.8 %reduce-scatter.7.cloned.1.call-start = ((), (), s32[]{:S(2)}) async-start(), calls=%async_computation.3 | async-start | bytes 2162688 | tf_op jit(solution)/shard_map/reduce_scatter | solution.py:147
  15.9 3.9 %copy-start.3 = (bf16[4096,128]{1,0:T(8,128)(2,1)}, bf16[4096,128]{1,0:T(8,128)(2,1)S(1)}, u32[]{:S(2)}) copy-start(bf16[4096,128]{1,0:T(8,128)(2,1)S(1)} %get-tuple-element.20) | copy-start | bytes 3145732
  26.2 133.0 %all-gather.3.cloned.1.call-start = ((), (), s32[]{:S(2)}) async-start(), calls=%async_computation.4 | async-start | bytes 2162688 | tf_op jit(solution)/shard_map/all_gather | solution.py:156
  107.0 4.7 %copy-start.8 = (bf16[4,64,64,128]{3,2,1,0:T(8,128)(2,1)S(1)}, bf16[4,64,64,128]{3,2,1,0:T(8,128)(2,1)}, u32[]{:S(2)}) copy-start(bf16[4,64,64,128]{3,2,1,0:T(8,128)(2,1)} %param.6) | copy-start | bytes 12582916
  113.8 152.2 %reduce-scatter.9.cloned.1.call-start = ((), (), s32[]{:S(2)}) async-start(), calls=%async_computation.5 | async-start | bytes 2162688 | tf_op jit(solution)/shard_map/reduce_scatter | solution.py:147
  163.9 2.2 copy-start.6
  163.9 3.5 copy-start.7
  167.3 10.5 %copy-start.4 = (bf16[4096,128]{1,0:T(8,128)(2,1)S(1)}, bf16[4096,128]{1,0:T(8,128)(2,1)}, u32[]{:S(2)}) copy-start(bf16[4096,128]{1,0:T(8,128)(2,1)} %copy-done.3) | copy-start | bytes 3145732
  175.8 2.0 copy-start.1
  189.6 130.6 %all-gather.5.cloned.1.call-start = ((), (), s32[]{:S(2)}) async-start(), calls=%async_computation.6 | async-start | bytes 2162688 | tf_op jit(solution)/shard_map/all_gather | solution.py:156
  266.0 5.8 %copy-start.5 = (bf16[4,64,128]{2,1,0:T(8,128)(2,1)S(1)}, bf16[4,64,128]{2,1,0:T(8,128)(2,1)}, u32[]{:S(2)}) copy-start(bf16[4,64,128]{2,1,0:T(8,128)(2,1)} %reduce-scatter.9.cloned.1.call-done) | copy-start | bytes 196612
  266.0 5.8 %copy-start.9 = (bf16[4,64,64,128]{3,2,1,0:T(8,128)(2,1)S(1)}, bf16[4,64,64,128]{3,2,1,0:T(8,128)(2,1)}, u32[]{:S(2)}) copy-start(bf16[4,64,64,128]{3,2,1,0:T(8,128)(2,1)} %param.6) | copy-start | bytes 12582916
  274.9 93.3 %reduce-scatter.11.cloned.1.call-start = ((), (), s32[]{:S(2)}) async-start(), calls=%async_computation.7 | async-start | bytes 5242880
  324.9 2.2 copy-start.2
Sparse Core Ops, SparseCore 0:
  26.3 80.6 reduce-scatter.6
  113.9 45.2 all-gather.2
  189.7 76.2 reduce-scatter.8
  275.0 45.1 all-gather.4
  322.5 45.6 reduce-scatter.10
where the time goes:
time: 378 us
  waiting for transfers between devices  265 us (70%)
  matrix products  43.6 us (12%)
  other arithmetic  32.6 us (9%)
  local copies, waits for them, and re-layouts  21.7 us (6%)
  between operations  14.1 us (4%)
    reduce_scatter x2, waiting for transfers between devices, to_modes(): lax.psum_scatter(row_forward(local_cos, local_sin, columns).astype(jnp.bf...  157 us
    all_gather x2, waiting for transfers between devices, to_rows(): lax.all_gather(spectrum, 'space', axis=0, tiled=True)  70.3 us
    unnamed x6, waiting for transfers between devices  37.9 us
    another operation x8, other arithmetic  18.6 us
    unnamed x23, local copies, waits for them, and re-layouts  12.6 us
    dot_general x1, matrix products, on_device(): jnp.einsum('rcn,cd->rdn', signal, mix_weight, preferred_element_type=jnp....  8.47 us
    concatenate x2, local copies, waits for them, and re-layouts, row_forward(): return jnp.concatenate([real_part, imag_part], axis=-1)  7.85 us
  transfers between devices with their start and end apart: 5, of which 5 were waited for; matrix products, arithmetic and copies ran while one was open for 8% of the time, Pallas kernels for 0%

commit v1 on v0

v1 whole, which is shorter than its diff:
```python
import math

import jax
import jax.numpy as jnp
import numpy as np
from jax import lax
from jax.sharding import PartitionSpec as P

GELU_CUBIC = 0.044715
GELU_SCALE = math.sqrt(2.0 / math.pi)


def gelu_value(values):
    inner_arg = GELU_SCALE * (values + GELU_CUBIC * values * values * values)
    return 0.5 * values * (1.0 + jnp.tanh(inner_arg))


def gelu_slope(values):
    tangent = jnp.tanh(GELU_SCALE * (values + GELU_CUBIC * values * values * values))
    return 0.5 * (1.0 + tangent) + 0.5 * values * (1.0 - tangent * tangent) * GELU_SCALE * (
        1.0 + 3.0 * GELU_CUBIC * values * values
    )


def trig(phase_index, period, extent):
    angles = phase_index.astype(np.float32) * np.float32(2.0 * math.pi / period)
    norm_scale = np.float32(1.0 / math.sqrt(extent))
    rounded = jnp.bfloat16
    return (
        (np.cos(angles) * norm_scale).astype(rounded),
        (np.sin(angles) * norm_scale).astype(rounded),
    )


def column_table(length, mode_count, owners):
    phase = np.arange(length)[:, None] * np.arange(mode_count)[None, :] % length
    cos_part, sin_part = trig(phase, length, length)
    both = np.stack([cos_part, -sin_part], axis=1)
    both = both.reshape(length, 2, owners, mode_count // owners)
    return both.transpose(0, 2, 1, 3).reshape(length, 2 * mode_count)


def column_weight(mode_count, owners):
    single = np.where(np.arange(mode_count) == 0, 1.0, 2.0).astype(np.float32)
    both = np.stack([single, single]).reshape(2, owners, mode_count // owners)
    return both.transpose(1, 0, 2).reshape(2 * mode_count)


def row_tables(extent, mode_count):
    slot = np.arange(mode_count)
    frequency = np.where(slot < mode_count // 2, slot, extent - mode_count + slot)
    phase = frequency[:, None] * np.arange(extent)[None, :] % extent
    return trig(phase, extent, extent)


def mix_modes(spectrum, weight):
    channels = weight.shape[2]
    real_prod = jnp.einsum(
        "ykc,ykcd->ykd", spectrum[..., :channels], weight, preferred_element_type=jnp.float32
    )
    imag_prod = jnp.einsum(
        "ykc,ykcd->ykd", spectrum[..., channels:], weight, preferred_element_type=jnp.float32
    )
    return jnp.concatenate(
        [
            real_prod[..., :channels] - imag_prod[..., channels:],
            real_prod[..., channels:] + imag_prod[..., :channels],
        ],
        axis=-1,
    )


def mix_adjoint(delta_modes, weight):
    channels = weight.shape[2]
    swapped = jnp.concatenate([delta_modes[..., channels:], -delta_modes[..., :channels]], axis=-1)
    first_half = jnp.einsum(
        "ykd,ykcd->ykc", delta_modes, weight, preferred_element_type=jnp.float32
    )
    second_half = jnp.einsum("ykd,ykcd->ykc", swapped, weight, preferred_element_type=jnp.float32)
    return jnp.concatenate([first_half, second_half], axis=-1)


def on_device(fields, cotangent, mode_weight, mix_weight):
    signal = fields[0]
    upstream = cotangent[0]
    rows_here, channels, length = signal.shape
    mode_rows, kx_count = mode_weight.shape[:2]
    groups = lax.axis_size("space")
    ky_count = mode_rows * groups
    extent = rows_here * groups
    table = jnp.asarray(column_table(length, ky_count, groups))
    weight = jnp.asarray(column_weight(ky_count, groups))
    row_cos, row_sin = row_tables(extent, kx_count)
    forward_rows = jnp.asarray(
        np.block([[row_cos, row_sin], [-row_sin, row_cos]]).reshape(
            2, kx_count, 2, groups, rows_here
        )
    )

    def exchange(values, axis):
        return lax.all_to_all(values, axis, 0, 0, tiled=True)

    def to_modes(columns):
        sent = columns.astype(jnp.bfloat16).reshape(groups, 2 * mode_rows, rows_here * channels)
        got = exchange(sent, "space").reshape(groups, 2, mode_rows, rows_here, channels)
        modes = jnp.einsum(
            "qjpsr,spirc->ijqc", forward_rows, got, preferred_element_type=jnp.float32
        )
        return modes.astype(jnp.bfloat16).reshape(mode_rows, kx_count, 2 * channels)

    def to_rows(modes):
        parts = modes.reshape(mode_rows, kx_count, 2, channels)
        back = jnp.einsum(
            "qjpsr,ijqc->spirc", forward_rows, parts, preferred_element_type=jnp.float32
        ).astype(jnp.bfloat16)
        sent = back.reshape(groups, 2 * mode_rows, rows_here * channels)
        return exchange(sent, "space").reshape(2 * ky_count, rows_here * channels)

    def by_kx(modes):
        samples = lax.axis_size("dp")
        parts = modes.reshape(mode_rows, samples, kx_count // samples, 2 * channels)
        return exchange(parts.transpose(1, 0, 2, 3), "dp")

    flat_signal = signal.reshape(rows_here * channels, length)
    columns = jnp.einsum("nm,xn->mx", table, flat_signal, preferred_element_type=jnp.float32)
    spectrum = to_modes(columns)
    modes_out = mix_modes(spectrum, mode_weight).astype(jnp.bfloat16)
    back_columns = to_rows(modes_out)
    spectral = jnp.einsum(
        "mx,nm->xn",
        back_columns * weight[:, None].astype(jnp.bfloat16),
        table,
        preferred_element_type=jnp.float32,
    ).reshape(rows_here, channels, length)
    preact = spectral + jnp.einsum(
        "rcn,cd->rdn", signal, mix_weight, preferred_element_type=jnp.float32
    )
    response = gelu_value(preact).astype(jnp.bfloat16)
    delta_field = (upstream.astype(jnp.float32) * gelu_slope(preact)).astype(jnp.bfloat16)
    delta_cols = (
        jnp.einsum(
            "nm,xn->mx",
            table,
            delta_field.reshape(rows_here * channels, length),
            preferred_element_type=jnp.float32,
        )
        * weight[:, None]
    )
    delta_modes = to_modes(delta_cols)
    input_modes = mix_adjoint(delta_modes, mode_weight).astype(jnp.bfloat16)
    input_cols = to_rows(input_modes)
    all_x = by_kx(spectrum)
    all_dy = by_kx(delta_modes)
    swapped = jnp.concatenate([all_dy[..., channels:], -all_dy[..., :channels]], axis=-1)
    mode_grad = jnp.einsum(
        "sykc,sykd->ykcd", all_x[..., :channels], all_dy, preferred_element_type=jnp.float32
    ) + jnp.einsum(
        "sykc,sykd->ykcd", all_x[..., channels:], swapped, preferred_element_type=jnp.float32
    )
    field_grad = jnp.einsum(
        "mx,nm->xn", input_cols, table, preferred_element_type=jnp.float32
    ).reshape(rows_here, channels, length)
    field_grad = field_grad + jnp.einsum(
        "rdn,cd->rcn", delta_field, mix_weight, preferred_element_type=jnp.float32
    )
    return (response[None], field_grad.astype(jnp.bfloat16)[None], mode_grad)


def solution(mesh):
    in_specs = (
        P("dp", "space", None, None),
        P("dp", "space", None, None),
        P("space", None, None, None),
        P(),
    )
    out_specs = (
        P("dp", "space", None, None),
        P("dp", "space", None, None),
        P("space", "dp", None, None),
    )
    return jax.shard_map(
        on_device, mesh=mesh, in_specs=in_specs, out_specs=out_specs, check_vma=False
    )
```

time: 378 us -> 117 us (0.31)
  waiting for transfers between devices: 265 us -> 26 us
  other arithmetic: 32.6 us -> 0.41 us
  starting transfers between devices: 0.61 us -> 21.4 us
  blocking collectives: 0 us -> 18.4 us
  between operations: 14.1 us -> 0.98 us
  local copies, waits for them, and re-layouts: 21.7 us -> 11.5 us
  matrix products: 43.6 us -> 38.2 us
    reduce_scatter x2 -> x0, waiting for transfers between devices: 157 us -> none  [to_modes(): lax.psum_scatter(row_forward(local_cos, local_sin, columns).astype(jnp.bf...]
    all_gather x2 -> x0, waiting for transfers between devices: 70.3 us -> none  [to_rows(): lax.all_gather(spectrum, 'space', axis=0, tiled=True)]
    unnamed x6 -> x0, waiting for transfers between devices: 37.9 us -> none
    all_to_all x0 -> x5, waiting for transfers between devices: none -> 26 us  [exchange(): return lax.all_to_all(values, axis, 0, 0, tiled=True)]
    all_to_all x0 -> x5, starting transfers between devices: none -> 21.4 us  [exchange(): return lax.all_to_all(values, axis, 0, 0, tiled=True)]
    another operation x12 -> x0, other arithmetic: 19.5 us -> none
    all_to_all x0 -> x1, blocking collectives: none -> 18.4 us  [exchange(): return lax.all_to_all(values, axis, 0, 0, tiled=True)]
    concatenate x2 -> x1, local copies, waits for them, and re-layouts: 7.85 us -> 0.13 us  [mix_adjoint(): jnp.concatenate([delta_modes[..., channels:], -delta_modes[..., :channels...]
  transfers between devices with their start and end apart: 5 -> 5, of which waited for: 5 -> 4; matrix products, arithmetic and copies ran while one was open for 8% -> 15% of each run, Pallas kernels for 0% -> 0%
where the time goes in v1:
time: 117 us
  matrix products  38.2 us (33%)
  waiting for transfers between devices  26 us (22%)
  starting transfers between devices  21.4 us (18%)
  blocking collectives  18.4 us (16%)
  local copies, waits for them, and re-layouts  11.5 us (10%)
    all_to_all x5, waiting for transfers between devices, exchange(): return lax.all_to_all(values, axis, 0, 0, tiled=True)  26 us
    all_to_all x5, starting transfers between devices, exchange(): return lax.all_to_all(values, axis, 0, 0, tiled=True)  21.4 us
    all_to_all x1, blocking collectives, exchange(): return lax.all_to_all(values, axis, 0, 0, tiled=True)  18.4 us
    dot_general x1, matrix products, on_device(): jnp.einsum('rcn,cd->rdn', signal, mix_weight, preferred_element_type=jnp....  8.47 us
    unnamed x28, local copies, waits for them, and re-layouts  5.1 us
    dot_general x1, matrix products, mix_adjoint(): jnp.einsum('ykd,ykcd->ykc', delta_modes, weight, preferred_element_type=j...  4.46 us
    dot_general x1, matrix products, mix_adjoint(): jnp.einsum('ykd,ykcd->ykc', swapped, weight, preferred_element_type=jnp.f...  4.43 us
    dot_general x1, matrix products, on_device(): jnp.einsum('nm,xn->mx', table, flat_signal, preferred_element_type=jnp.fl...  4.16 us
  transfers between devices with their start and end apart: 5, of which 4 were waited for; matrix products, arithmetic and copies ran while one was open for 15% of the time, Pallas kernels for 0%

profile of v1, /device:TPU:1, one launch (start us, length us, event | category | flops | bytes accessed | tf_op | source)
XLA Modules:
  0.0 116.8 jit_solution(16521926738486902054)
XLA Ops:
  0.7 4.2 %fusion.17 = bf16[32,8,512]{2,1,0:T(8,128)(2,1)S(1)} fusion(bf16[4096,256]{1,0:T(8,128)(2,1)} %constant.16.clone, bf16[512,4096]{1,0:T(8,128)(2,1)} %bitcast.171), kind=kOutput, calls=%fused_computation.29 | convolution fusion | flops 1073872896 | bytes 6553600 | tf_op jit(solution)/shard_map/nm,xn->mx/dot_general | solution.py:125
  4.8 18.4 %all_to_all.30 = bf16[32,8,512]{2,1,0:T(8,128)(2,1)S(1)} all-to-all(bf16[32,8,512]{2,1,0:T(8,128)(2,1)S(1)} %fusion.17), channel_id=1, replica_groups=mesh['dp'=4,'space'=32] {'space'}, dimensions={0} | all-to-all | bytes 524288 | tf_op jit(solution)/shard_map/all_to_all | solution.py:101
  24.3 3.5 %fusion.51 = f32[4,64,1,128]{3,2,1,0:T(1,128)S(1)} fusion(bf16[4,64,64,1]{2,3,1,0:T(2,128)(2,1)S(1)} %copy.67, bf16[4,64,64,128]{3,2,1,0:T(8,128)(2,1)} %param.9), kind=kOutput, calls=%fused_computation.71 | convolution fusion | flops 4194304 | bytes 4358144 | tf_op jit(solution)/shard_map/ykc,ykcd->ykd/dot_general | solution.py:61
  27.8 1.2 %fusion.50 = f32[4,64,1,128]{3,2,1,0:T(1,128)S(1)} fusion(bf16[4,64,64,1]{2,3,1,0:T(2,128)(2,1)S(1)} %copy.65, bf16[4,64,64,128]{3,2,1,0:T(8,128)(2,1)S(1)} %copy-done.11), kind=kOutput, calls=%fused_computation.70 | convolution fusion | flops 4194304 | bytes 4358144 | tf_op jit(solution)/shard_map/ykc,ykcd->ykd/dot_general | solution.py:58
  29.8 1.0 reshape.61
  30.8 3.7 %all-to-all-start.1 = ((bf16[32,8,512]{2,1,0:T(8,128)(2,1)}), bf16[32,8,512]{2,1,0:T(8,128)(2,1)S(1)}, u32[]{:S(2)}, u32[]{:S(2)}) async-start(bf16[32,8,512]{2,1,0:T(8,128)(2,1)} %reshape.61), calls=%async_computation.1 | async-start | bytes 524288 | tf_op jit(solution)/shard_map/all_to_all | solution.py:101
  35.4 8.2 %all-to-all-done.1 = bf16[32,8,512]{2,1,0:T(8,128)(2,1)S(1)} async-done(((bf16[32,8,512]{2,1,0:T(8,128)(2,1)}), bf16[32,8,512]{2,1,0:T(8,128)(2,1)S(1)}, u32[]{:S(2)}, u32[]{:S(2)}) %all-to-all-start.1) | async-done | bytes 262176 | tf_op jit(solution)/shard_map/all_to_all | solution.py:101
  43.6 4.0 %all-to-all-start.4 = ((bf16[4,4,16,128]{3,2,1,0:T(8,128)(2,1)}), bf16[4,4,16,128]{3,2,1,0:T(8,128)(2,1)S(1)}, u32[]{:S(2)}, u32[]{:S(2)}) async-start(bf16[4,4,16,128]{3,2,1,0:T(8,128)(2,1)} %copy.55), calls=%async_computation.4 | async-start | bytes 131072 | tf_op jit(solution)/shard_map/all_to_all | solution.py:101
  47.9 1.3 %fusion.52 = f32[8,64,4096]{2,1,0:T(8,128)S(1)} fusion(bf16[8,64,256]{2,1,0:T(8,128)(2,1)S(1)} %bitcast.164, bf16[4096,256,1]{1,0,2:T(8,128)(2,1)S(1)} %copy-done.1), kind=kOutput, calls=%fused_computation.72 | convolution fusion | flops 1073741824 | bytes 10747904 | tf_op jit(solution)/shard_map/mx,nm->xn/dot_general | solution.py:129
  50.1 1.3 %copy-done.10 = bf16[1,8,64,4096]{3,2,1,0:T(8,128)(2,1)S(1)} copy-done((bf16[1,8,64,4096]{3,2,1,0:T(8,128)(2,1)S(1)}, bf16[1,8,64,4096]{3,2,1,0:T(8,128)(2,1)}, u32[]{:S(2)}) %copy-start.10) | copy-done | bytes 4194328
  51.4 8.5 %fusion.6 = (bf16[8,64,4096]{2,1,0:T(8,128)(2,1)S(1)}, bf16[1,8,64,4096]{3,2,1,0:T(8,128)(2,1)}) fusion(bf16[1,8,64,4096]{3,2,1,0:T(8,128)(2,1)S(1)} %copy-done.9, f32[8,64,4096]{2,1,0:T(8,128)S(1)} %fusion.52, bf16[1,8,64,4096]{3,2,1,0:T(8,128)(2,1)S(1)} %copy-done.10, bf16[64,64]{1,0:T(8,128)(2,1)S(1)} %copy-done), kind=kOutput, calls=%fused_computation.8 | convolution fusion | flops 316669952 | bytes 25174016 | tf_op jit(solution)/shard_map/rcn,cd->rdn/dot_general | solution.py:135
  59.9 2.0 %copy-done.2 = bf16[8,64,4096]{2,1,0:T(8,128)(2,1)} copy-done((bf16[8,64,4096]{2,1,0:T(8,128)(2,1)}, bf16[8,64,4096]{2,1,0:T(8,128)(2,1)S(1)}, u32[]{:S(2)}) %copy-start.2) | copy-done | bytes 4194328
  61.9 2.0 %fusion.16 = bf16[32,8,512]{2,1,0:T(8,128)(2,1)} fusion(bf16[512,4096]{1,0:T(8,128)(2,1)S(1)} %bitcast.154, bf16[4096,256]{1,0:T(8,128)(2,1)S(1)} %copy-done.12, f32[256]{0:T(256)S(1)} %copy-done.13), kind=kOutput, calls=%fused_computation.26 | convolution fusion | flops 1074003968 | bytes 6554624 | tf_op jit(solution)/shard_map/nm,xn->mx/dot_general | solution.py:141
  63.9 4.0 %all-to-all-start.2 = ((bf16[32,8,512]{2,1,0:T(8,128)(2,1)}), bf16[32,8,512]{2,1,0:T(8,128)(2,1)S(1)}, u32[]{:S(2)}, u32[]{:S(2)}) async-start(bf16[32,8,512]{2,1,0:T(8,128)(2,1)} %fusion.16), calls=%async_computation.2 | async-start | bytes 524288 | tf_op jit(solution)/shard_map/all_to_all | solution.py:101
  68.6 8.4 %all-to-all-done.2 = bf16[32,8,512]{2,1,0:T(8,128)(2,1)S(1)} async-done(((bf16[32,8,512]{2,1,0:T(8,128)(2,1)}), bf16[32,8,512]{2,1,0:T(8,128)(2,1)S(1)}, u32[]{:S(2)}, u32[]{:S(2)}) %all-to-all-start.2) | async-done | bytes 262176 | tf_op jit(solution)/shard_map/all_to_all | solution.py:101
  78.0 4.4 %fusion.54 = f32[4,64,1,64]{3,2,1,0:T(1,128)S(1)} fusion(bf16[4,64,128,1]{2,3,1,0:T(2,128)(2,1)S(1)} %copy.76, bf16[4,64,64,128]{3,2,1,0:T(8,128)(2,1)} %param.9), kind=kOutput, calls=%fused_computation.74 | convolution fusion | flops 4194304 | bytes 4325376 | tf_op jit(solution)/shard_map/ykd,ykcd->ykc/dot_general | solution.py:79
  82.6 4.5 %fusion.53 = f32[4,64,1,64]{3,2,1,0:T(1,128)S(1)} fusion(bf16[4,64,128,1]{2,3,1,0:T(2,128)(2,1)S(1)} %copy.74, bf16[4,64,64,128]{3,2,1,0:T(8,128)(2,1)} %param.9), kind=kOutput, calls=%fused_computation.73 | convolution fusion | flops 4194304 | bytes 4325376 | tf_op jit(solution)/shard_map/ykd,ykcd->ykc/dot_general | solution.py:76
  88.0 4.5 %all-to-all-start.5 = ((bf16[4,4,16,128]{3,2,1,0:T(8,128)(2,1)}), bf16[4,4,16,128]{3,2,1,0:T(8,128)(2,1)S(1)}, u32[]{:S(2)}, u32[]{:S(2)}) async-start(bf16[4,4,16,128]{3,2,1,0:T(8,128)(2,1)} %copy.58), calls=%async_computation.5 | async-start | bytes 131072 | tf_op jit(solution)/shard_map/all_to_all | solution.py:101
  94.1 2.9 %all-to-all-done.5 = bf16[4,4,16,128]{3,2,1,0:T(8,128)(2,1)S(1)} async-done(((bf16[4,4,16,128]{3,2,1,0:T(8,128)(2,1)}), bf16[4,4,16,128]{3,2,1,0:T(8,128)(2,1)S(1)}, u32[]{:S(2)}, u32[]{:S(2)}) %all-to-all-start.5) | async-done | bytes 65568 | tf_op jit(solution)/shard_map/all_to_all | solution.py:101
  96.9 5.1 %all-to-all-start.3 = ((bf16[32,8,512]{2,1,0:T(8,128)(2,1)}), bf16[32,8,512]{2,1,0:T(8,128)(2,1)S(1)}, u32[]{:S(2)}, u32[]{:S(2)}) async-start(bf16[32,8,512]{2,1,0:T(8,128)(2,1)} %reshape.67), calls=%async_computation.3 | async-start | bytes 524288 | tf_op jit(solution)/shard_map/all_to_all | solution.py:101
  102.8 1.9 %convolution_add_fusion = f32[4,16,64,128]{3,2,1,0:T(8,128)} fusion(f32[4,16,64,128]{3,2,1,0:T(8,128)S(1)} %fusion.35, bf16[4,4,16,64]{3,0,2,1:T(4,128)(2,1)S(1)} %get-tuple-element.14, bf16[4,4,16,64]{3,0,2,1:T(4,128)(2,1)S(1)} %get-tuple-element.13, bf16[4,4,16,64]{3,2,1,0:T(8,128)(2,1)S(1)} %copy-done.6), kind=kOutput, calls=%fused_computation.16 | convolution fusion | flops 4849664 | bytes 4292608 | tf_op jit(solution)/shard_map/sykc,sykd->ykcd/dot_general | solution.py:157
  104.6 6.6 %all-to-all-done.3 = bf16[32,8,512]{2,1,0:T(8,128)(2,1)S(1)} async-done(((bf16[32,8,512]{2,1,0:T(8,128)(2,1)}), bf16[32,8,512]{2,1,0:T(8,128)(2,1)S(1)}, u32[]{:S(2)}, u32[]{:S(2)}) %all-to-all-start.3) | async-done | bytes 262176 | tf_op jit(solution)/shard_map/all_to_all | solution.py:101
  111.3 1.3 %fusion.55 = f32[8,64,4096]{2,1,0:T(8,128)S(1)} fusion(bf16[8,64,256]{2,1,0:T(8,128)(2,1)S(1)} %bitcast.163, bf16[4096,256,1]{1,0,2:T(8,128)(2,1)S(1)} %copy-done.1), kind=kOutput, calls=%fused_computation.75 | convolution fusion | flops 1073741824 | bytes 10747904 | tf_op jit(solution)/shard_map/mx,nm->xn/dot_general | solution.py:160
  113.5 3.3 %fusion.8 = bf16[1,8,64,4096]{3,2,1,0:T(8,128)(2,1)} fusion(f32[8,64,4096]{2,1,0:T(8,128)S(1)} %fusion.55, bf16[8,64,4096]{2,1,0:T(8,128)(2,1)S(1)} %copy-done.3, bf16[64,64]{1,0:T(8,128)(2,1)S(1)} %copy-done), kind=kOutput, calls=%fused_computation.13 | convolution fusion | flops 272629760 | bytes 16785408 | tf_op jit(solution)/shard_map/rdn,cd->rcn/dot_general | solution.py:163
  (58 shorter events, 9.8 us)
Async XLA Ops:
  0.6 48.6 %copy-start = (bf16[64,64]{1,0:T(8,128)(2,1)S(1)}, bf16[64,64]{1,0:T(8,128)(2,1)}, u32[]{:S(2)}) copy-start(bf16[64,64]{1,0:T(8,128)(2,1)} %param.10) | copy-start | bytes 24580
  0.6 22.9 %copy-start.5 = (bf16[2,64,2,32,8,1]{1,3,4,2,0,5:T(8,128)(2,1)S(1)}, bf16[2,64,2,32,8,1]{1,3,4,2,0,5:T(8,128)(2,1)}, u32[]{:S(2)}) copy-start(bf16[2,64,2,32,8,1]{1,3,4,2,0,5:T(8,128)(2,1)} %constant.23) | copy-start | bytes 393220
  24.3 3.5 %copy-start.11 = (bf16[4,64,64,128]{3,2,1,0:T(8,128)(2,1)S(1)}, bf16[4,64,64,128]{3,2,1,0:T(8,128)(2,1)}, u32[]{:S(2)}) copy-start(bf16[4,64,64,128]{3,2,1,0:T(8,128)(2,1)} %param.9) | copy-start | bytes 12582916
  27.8 1.4 %copy-start.4 = (bf16[2,64,2,32,8,1]{1,3,0,4,2,5:T(8,128)(2,1)S(1)}, bf16[2,64,2,32,8,1]{1,3,0,4,2,5:T(8,128)(2,1)}, u32[]{:S(2)}) copy-start(bf16[2,64,2,32,8,1]{1,3,0,4,2,5:T(8,128)(2,1)} %constant.25) | copy-start | bytes 393220
  27.8 19.8 %copy-start.8 = (bf16[256]{0:T(256)(128)(2,1)S(1)}, bf16[256]{0:T(256)(128)(2,1)}, u32[]{:S(2)}) copy-start(bf16[256]{0:T(256)(128)(2,1)} %constant.22) | copy-start | bytes 1540
  29.1 18.8 %copy-start.1 = (bf16[4096,256,1]{1,0,2:T(8,128)(2,1)S(1)}, bf16[4096,256,1]{1,0,2:T(8,128)(2,1)}, u32[]{:S(2)}) copy-start(bf16[4096,256,1]{1,0,2:T(8,128)(2,1)} %constant.26) | copy-start | bytes 6291460
  30.8 12.8 %all-to-all-start.1 = ((bf16[32,8,512]{2,1,0:T(8,128)(2,1)}), bf16[32,8,512]{2,1,0:T(8,128)(2,1)S(1)}, u32[]{:S(2)}, u32[]{:S(2)}) async-start(bf16[32,8,512]{2,1,0:T(8,128)(2,1)} %reshape.61), calls=%async_computation.1 | async-start | bytes 524288 | tf_op jit(solution)/shard_map/all_to_all | solution.py:101
  43.6 20.2 %all-to-all-start.4 = ((bf16[4,4,16,128]{3,2,1,0:T(8,128)(2,1)}), bf16[4,4,16,128]{3,2,1,0:T(8,128)(2,1)S(1)}, u32[]{:S(2)}, u32[]{:S(2)}) async-start(bf16[4,4,16,128]{3,2,1,0:T(8,128)(2,1)} %copy.55), calls=%async_computation.4 | async-start | bytes 131072 | tf_op jit(solution)/shard_map/all_to_all | solution.py:101
  47.9 2.2 %copy-start.9 = (bf16[1,8,64,4096]{3,2,1,0:T(8,128)(2,1)S(1)}, bf16[1,8,64,4096]{3,2,1,0:T(8,128)(2,1)}, u32[]{:S(2)}) copy-start(bf16[1,8,64,4096]{3,2,1,0:T(8,128)(2,1)} %param.8) | copy-start | bytes 12582916
  47.9 3.5 %copy-start.10 = (bf16[1,8,64,4096]{3,2,1,0:T(8,128)(2,1)S(1)}, bf16[1,8,64,4096]{3,2,1,0:T(8,128)(2,1)}, u32[]{:S(2)}) copy-start(bf16[1,8,64,4096]{3,2,1,0:T(8,128)(2,1)} %param.7) | copy-start | bytes 12582916
  51.4 10.5 %copy-start.12 = (bf16[4096,256]{1,0:T(8,128)(2,1)S(1)}, bf16[4096,256]{1,0:T(8,128)(2,1)}, u32[]{:S(2)}) copy-start(bf16[4096,256]{1,0:T(8,128)(2,1)} %constant.16.clone) | copy-start | bytes 6291460
  51.4 10.5 %copy-start.13 = (f32[256]{0:T(256)S(1)}, f32[256]{0:T(256)}, u32[]{:S(2)}) copy-start(f32[256]{0:T(256)} %constant.17.clone) | copy-start | bytes 3076
  59.9 2.0 %copy-start.2 = (bf16[8,64,4096]{2,1,0:T(8,128)(2,1)}, bf16[8,64,4096]{2,1,0:T(8,128)(2,1)S(1)}, u32[]{:S(2)}) copy-start(bf16[8,64,4096]{2,1,0:T(8,128)(2,1)S(1)} %get-tuple-element.3) | copy-start | bytes 12582916
  63.9 13.1 %all-to-all-start.2 = ((bf16[32,8,512]{2,1,0:T(8,128)(2,1)}), bf16[32,8,512]{2,1,0:T(8,128)(2,1)S(1)}, u32[]{:S(2)}, u32[]{:S(2)}) async-start(bf16[32,8,512]{2,1,0:T(8,128)(2,1)} %fusion.16), calls=%async_computation.2 | async-start | bytes 524288 | tf_op jit(solution)/shard_map/all_to_all | solution.py:101
  82.6 19.7 %copy-start.7 = (bf16[4,4,16,64]{3,2,1,0:T(8,128)(2,1)S(1)}, bf16[4,4,16,64]{3,2,1,0:T(8,128)(2,1)}, u32[]{:S(2)}) copy-start(bf16[4,4,16,64]{3,2,1,0:T(8,128)(2,1)} %get-tuple-element.12) | copy-start | bytes 98308
  87.0 15.7 %copy-start.6 = (bf16[4,4,16,64]{3,2,1,0:T(8,128)(2,1)S(1)}, bf16[4,4,16,64]{3,2,1,0:T(8,128)(2,1)}, u32[]{:S(2)}) copy-start(bf16[4,4,16,64]{3,2,1,0:T(8,128)(2,1)} %get-tuple-element.11) | copy-start | bytes 98308
  88.0 9.0 %all-to-all-start.5 = ((bf16[4,4,16,128]{3,2,1,0:T(8,128)(2,1)}), bf16[4,4,16,128]{3,2,1,0:T(8,128)(2,1)S(1)}, u32[]{:S(2)}, u32[]{:S(2)}) async-start(bf16[4,4,16,128]{3,2,1,0:T(8,128)(2,1)} %copy.58), calls=%async_computation.5 | async-start | bytes 131072 | tf_op jit(solution)/shard_map/all_to_all | solution.py:101
  96.9 14.2 %all-to-all-start.3 = ((bf16[32,8,512]{2,1,0:T(8,128)(2,1)}), bf16[32,8,512]{2,1,0:T(8,128)(2,1)S(1)}, u32[]{:S(2)}, u32[]{:S(2)}) async-start(bf16[32,8,512]{2,1,0:T(8,128)(2,1)} %reshape.67), calls=%async_computation.3 | async-start | bytes 524288 | tf_op jit(solution)/shard_map/all_to_all | solution.py:101
  111.3 2.2 %copy-start.3 = (bf16[8,64,4096]{2,1,0:T(8,128)(2,1)S(1)}, bf16[8,64,4096]{2,1,0:T(8,128)(2,1)}, u32[]{:S(2)}) copy-start(bf16[8,64,4096]{2,1,0:T(8,128)(2,1)} %copy-done.2) | copy-start | bytes 12582916

commit v2 on v1

v2 whole, which is shorter than its diff:
```python
import math

import jax
import jax.numpy as jnp
import numpy as np
from jax import lax
from jax.experimental import pallas as pl
from jax.experimental.pallas import tpu as pltpu
from jax.sharding import PartitionSpec as P

GELU_CUBIC = 0.044715
GELU_SCALE = math.sqrt(2.0 / math.pi)
LANES = 128
BF16 = jnp.bfloat16
F32 = jnp.float32
STACK = 4
TILE = 512
DIAGONAL = 256
AHEAD = 3
MIB = 1024 * 1024


def trig(phase_index, extent):
    angles = phase_index.astype(np.float32) * np.float32(2.0 * math.pi / extent)
    norm_scale = np.float32(1.0 / math.sqrt(extent))
    return (
        (np.cos(angles) * norm_scale).astype(BF16).astype(np.float32),
        (np.sin(angles) * norm_scale).astype(BF16).astype(np.float32),
    )


def column_table(length, mode_count, owners):
    phase = np.arange(mode_count)[:, None] * np.arange(length)[None, :] % length
    cos_part, sin_part = trig(phase, length)
    both = np.stack([cos_part, -sin_part]).reshape(2, owners, mode_count // owners, length)
    return both.transpose(1, 0, 2, 3).reshape(2 * mode_count, length).astype(BF16)


def row_matrix(extent, mode_count):
    slot = np.arange(mode_count)
    frequency = np.where(slot < mode_count // 2, slot, extent - mode_count + slot)
    phase = frequency[:, None] * np.arange(extent)[None, :] % extent
    cos_part, sin_part = trig(phase, extent)
    return np.stack(
        [np.stack([cos_part, sin_part], 1), np.stack([-sin_part, cos_part], 1)], 1
    )


def split_rows(matrix, owners):
    rows, parts, extent = matrix.shape
    split = matrix.reshape(rows, parts, owners, extent // owners // 2, 2)
    split = split.transpose(4, 0, 1, 3, 2)
    return split.reshape(2, rows, parts * extent // 2)


def half_mask(shape):
    return lax.broadcasted_iota(jnp.int32, shape, len(shape) - 1) % LANES < LANES // 2


def fold(first, second):
    picked = jnp.where(half_mask(first.shape), first, second)
    return picked + pltpu.roll(picked, LANES // 2, 1)


def dot_nt(left, right):
    return lax.dot_general(left, right, (((1,), (1,)), ((), ())), preferred_element_type=F32)


def dot_nn(left, right):
    return jnp.dot(left, right, preferred_element_type=F32)


def weigh(values, mode_rows):
    row = lax.broadcasted_iota(jnp.int32, values.shape, 0)
    return jnp.where((row == 0) | (row == mode_rows), values, values * 2.0)


def tiles(length):
    return [slice(at, at + TILE) for at in range(0, length, TILE)]


class Loads:
    def __init__(self, pairs, sem_ref, ahead):
        self.copies = [
            [
                pltpu.make_async_copy(source.at[:, cols], target.at[:, cols], sem_ref.at[n, k])
                for n, (source, target) in enumerate(pairs)
            ]
            for k, cols in enumerate(tiles(pairs[0][0].shape[1]))
        ]
        self.ahead = ahead
        for k in range(ahead):
            self.start(k)

    def start(self, k):
        if k < len(self.copies):
            for copy in self.copies[k]:
                copy.start()

    def wait(self, k):
        for copy in self.copies[k]:
            copy.wait()
        self.start(k + self.ahead)


def columns_kernel(table_hbm, fields_hbm, out_ref, fields_ref, table_ref, acc_ref, sem_ref):
    parts = tiles(table_hbm.shape[1])
    loads = Loads(((table_hbm, table_ref), (fields_hbm, fields_ref)), sem_ref, AHEAD)
    for k, cols in enumerate(parts):
        loads.wait(k)
        product = dot_nt(table_ref[:, cols], fields_ref[:, cols])
        if k == 0:
            acc_ref[...] = product
        elif k < len(parts) - 1:
            acc_ref[...] += product
        else:
            out_ref[...] = (acc_ref[...] + product).reshape(out_ref.shape).astype(BF16)


def gather_rows(got_ref, flat_ref, z_ref):
    owners, slots, width = got_ref.shape
    mode_rows = slots // 2
    for h in range(width // LANES):
        part = got_ref[:, :, h * LANES : (h + 1) * LANES].astype(F32)
        flat_ref[h] = part.reshape(owners * slots, LANES)
    for p in range(2):
        for i in range(mode_rows):
            for h in range(width // LANES):
                block = flat_ref[h, pl.ds(p * mode_rows + i, owners, stride=slots), :]
                at = (p * (width // LANES) + h) * owners
                z_ref[i, at : at + owners, :] = block.astype(BF16)


def scatter_rows(values, flat_ref, i, owners, slots):
    mode_rows = slots // 2
    columns = flat_ref.shape[0]
    for p in range(2):
        for h in range(columns):
            at = (p * columns + h) * owners
            flat_ref[h, pl.ds(p * mode_rows + i, owners, stride=slots), :] = values[
                at : at + owners
            ]


def modes_kernel(
    place_ref, got_ref, weight_ref, rows_ref, back_ref, *rest, adjoint, samples
):
    given = samples if adjoint else 0
    x_refs, sent_ref, shared_refs = rest[:given], rest[given], rest[given + 1 : given + 1 + samples]
    flat_ref, z_ref, mode_ref, y_ref = rest[given + 1 + samples :]
    owners, slots, _ = got_ref.shape
    mode_rows, kx_count, channels, _ = weight_ref.shape
    gather_rows(got_ref, flat_ref, z_ref)
    count = 2 * kx_count
    stack_rows = 2 * STACK
    for i in range(mode_rows):
        z = z_ref[i]
        both = fold(dot_nn(rows_ref[0], z), dot_nn(rows_ref[1], z))
        if adjoint:
            plain, turned = both[:count], both[count:]
            left = jnp.where(half_mask(plain.shape), plain, turned)
            mode_ref[i] = left
            left = left.astype(BF16)
            row = lax.broadcasted_iota(jnp.int32, (stack_rows, LANES), 0) // 2
            low = half_mask((stack_rows, LANES))
            for g in range(kx_count // STACK):
                pair = left[g // 2 * 2 * stack_rows : (g // 2 + 1) * 2 * stack_rows]
                w = weight_ref[i, g * STACK : (g + 1) * STACK].reshape(STACK * channels, LANES)
                full = dot_nt(pair, w)[g % 2 * stack_rows : (g % 2 + 1) * stack_rows]
                picked = jnp.where(row < 2, full[:, :LANES], full[:, LANES:])
                picked = jnp.where((row % 2 == 0) == low, picked, 0.0)
                y_ref[g * stack_rows : (g + 1) * stack_rows, :] = picked + pltpu.roll(
                    picked, LANES // 2, 1
                )
        else:
            wide = jnp.concatenate([both, both], axis=1)
            lane = lax.broadcasted_iota(jnp.int32, wide.shape, 1) // channels
            row = lax.broadcasted_iota(jnp.int32, wide.shape, 0) % stack_rows // 2
            left = jnp.where(lane == row, wide, 0.0).astype(BF16)
            for g in range(kx_count // STACK):
                rows = slice(g * 2 * stack_rows, (g + 1) * 2 * stack_rows)
                mode_ref[i, g * stack_rows : (g + 1) * stack_rows, :] = both[rows][:stack_rows]
                w = weight_ref[i, g * STACK : (g + 1) * STACK].reshape(STACK * channels, LANES)
                full = dot_nn(left[rows], w)
                y_ref[g * stack_rows : (g + 1) * stack_rows, :] = fold(
                    full[:stack_rows], full[stack_rows:]
                )
        y = y_ref[...].astype(BF16)
        low = half_mask((back_ref.shape[1], LANES))
        values = jnp.where(low, dot_nn(back_ref[0], y), dot_nn(back_ref[1], y))
        scatter_rows(values, flat_ref, i, owners, slots)
    for h in range(flat_ref.shape[0]):
        part = flat_ref[h].reshape(owners, slots, LANES)
        sent_ref[:, :, h * LANES : (h + 1) * LANES] = part.astype(BF16)
    block = count // samples
    for k, shared_ref in enumerate(shared_refs):
        start = pl.multiple_of((place_ref[0] + k) % samples * block, block)
        if adjoint:
            shared_ref[0] = x_refs[k][...]
        for i in range(mode_rows):
            values = mode_ref[i, pl.ds(start, block), :].astype(BF16)
            if adjoint:
                shared_ref[1, i] = values
            else:
                shared_ref[i] = values


def transposed_back(back_ref, mode_rows, weighted):
    owners, slots, width = back_ref.shape
    flat = back_ref[...].astype(F32).reshape(owners * slots, width)
    if weighted:
        flat = weigh(flat, mode_rows)
    return flat.T.astype(BF16)


def spread(block, out_ref):
    out_ref[...] = jnp.zeros_like(out_ref)
    size = block.shape[0]
    for at in range(0, out_ref.shape[0], size):
        out_ref[at : at + size, at : at + size] = block


def field_kernel(
    back_ref, table_ref, fields_ref, upstream_hbm, weight_ref,
    response_hbm, delta_hbm, sent_ref,
    upstream_ref, response_ref, delta_ref, turned_ref, mix_ref, pre_ref, acc_ref, sem_ref,
):
    loads = Loads(((upstream_hbm, upstream_ref),), sem_ref, AHEAD)
    mode_rows = back_ref.shape[1] // 2
    turned_ref[...] = transposed_back(back_ref, mode_rows, True)
    spread(weight_ref[...].astype(F32).T.astype(BF16), mix_ref)
    width = mix_ref.shape[0]
    total = fields_ref.shape[0]
    chunk = 32
    parts = tiles(table_ref.shape[1])
    copies = []
    for k, cols in enumerate(parts):
        slot = k % pre_ref.shape[0]
        for at in range(0, total, width):
            rows = slice(at, at + width)
            pre_ref[slot, rows, :] = dot_nn(turned_ref[rows, :], table_ref[:, cols]) + dot_nn(
                mix_ref[...], fields_ref[rows, cols]
            )
        loads.wait(k)
        for at in range(0, total, chunk):
            rows = slice(at, at + chunk)
            v = pre_ref[slot, rows, :]
            square = v * v
            half = 0.5 + 0.5 * jnp.tanh(v * (GELU_SCALE + (GELU_SCALE * GELU_CUBIC) * square))
            value = v * half
            response_ref[rows, cols] = value.astype(BF16)
            slope = half + value * (1.0 - half) * (
                2.0 * GELU_SCALE + (6.0 * GELU_SCALE * GELU_CUBIC) * square
            )
            delta_ref[rows, cols] = (upstream_ref[rows, cols].astype(F32) * slope).astype(BF16)
        for n, (source, target) in enumerate(
            ((response_ref, response_hbm), (delta_ref, delta_hbm))
        ):
            copies.append(
                pltpu.make_async_copy(
                    source.at[:, cols], target.at[:, cols], sem_ref.at[1 + n, k]
                )
            )
            copies[-1].start()
        product = dot_nt(table_ref[:, cols], delta_ref[:, cols])
        if k == 0:
            acc_ref[...] = product
        elif k < len(parts) - 1:
            acc_ref[...] += product
        else:
            sent = weigh(acc_ref[...] + product, mode_rows)
            sent_ref[...] = sent.reshape(sent_ref.shape).astype(BF16)
    for copy in copies:
        copy.wait()


def grad_kernel(
    back_ref, table_ref, delta_hbm, weight_ref, out_hbm,
    delta_ref, turned_ref, mix_ref, out_ref, sem_ref,
):
    loads = Loads(((delta_hbm, delta_ref),), sem_ref, AHEAD)
    turned_ref[...] = transposed_back(back_ref, 0, False)
    spread(weight_ref[...], mix_ref)
    width = mix_ref.shape[0]
    copies = []
    for k, cols in enumerate(tiles(table_ref.shape[1])):
        loads.wait(k)
        for at in range(0, delta_ref.shape[0], width):
            rows = slice(at, at + width)
            out_ref[rows, cols] = (
                dot_nn(turned_ref[rows, :], table_ref[:, cols])
                + dot_nn(mix_ref[...], delta_ref[rows, cols])
            ).astype(BF16)
        copy = pltpu.make_async_copy(out_ref.at[:, cols], out_hbm.at[:, cols], sem_ref.at[1, k])
        copy.start()
        copies.append(copy)
    for copy in copies:
        copy.wait()


def mode_grad_kernel(*refs, samples):
    shared_refs, out_ref = refs[:samples], refs[samples]
    mode_rows, kx_here, channels, _ = out_ref.shape
    stack_rows = 2 * STACK
    count = samples * stack_rows
    row = lax.broadcasted_iota(jnp.int32, (count, LANES), 0) % stack_rows // 2
    for i in range(mode_rows):
        for g in range(kx_here // STACK):
            rows = slice(g * stack_rows, (g + 1) * stack_rows)
            x = jnp.concatenate([ref[0, i, rows, :].astype(F32) for ref in shared_refs], axis=0)
            d = jnp.concatenate([ref[1, i, rows, :].astype(F32) for ref in shared_refs], axis=0)
            wide = jnp.concatenate(
                [jnp.where(row == m, d, 0.0) for m in range(STACK)], axis=1
            ).astype(BF16)
            turned = x.T[:channels].astype(BF16)
            product = dot_nn(turned, wide)
            for m in range(STACK):
                out_ref[i, g * STACK + m] = product[:, m * LANES : (m + 1) * LANES]


VMEM = pl.BlockSpec(memory_space=pltpu.VMEM)
HBM = pl.BlockSpec(memory_space=pltpu.HBM)


def pinned(values):
    return pltpu.with_memory_space_constraint(values, pltpu.HBM)


def params(mib):
    return pltpu.CompilerParams(vmem_limit_bytes=mib * MIB)


def on_device(fields, cotangent, mode_weight, mix_weight):
    _, rows_here, channels, length = fields.shape
    mode_rows, kx_count = mode_weight.shape[:2]
    groups = lax.axis_size("space")
    samples = lax.axis_size("dp")
    ky_count = mode_rows * groups
    extent = rows_here * groups
    lines = rows_here * channels
    slots = 2 * mode_rows
    signal = fields.reshape(lines, length)
    upstream = cotangent.reshape(lines, length)
    table = jnp.asarray(column_table(length, ky_count, groups))
    matrix = row_matrix(extent, kx_count)
    turned = np.stack([-matrix[:, 1], matrix[:, 0]], 1)
    plain_rows = matrix.reshape(2 * kx_count, 2, extent)
    turned_rows = turned.reshape(2 * kx_count, 2, extent)
    grouped = np.concatenate(
        [
            part.reshape(kx_count // STACK, 2 * STACK, 2, extent)
            for part in (plain_rows, turned_rows)
        ],
        axis=1,
    ).reshape(4 * kx_count, 2, extent)
    mix_rows = jnp.asarray(split_rows(grouped, groups).astype(BF16))
    adjoint_rows = jnp.asarray(
        split_rows(np.concatenate([plain_rows, -turned_rows]), groups).astype(BF16)
    )
    back_rows = jnp.asarray(
        split_rows(plain_rows, groups).transpose(0, 2, 1).astype(BF16)
    )
    place = lax.axis_index("dp").astype(jnp.int32).reshape(1)

    exchange_shape = jax.ShapeDtypeStruct((groups, slots, lines), BF16)
    lines_shape = pltpu.HBM((lines, length), BF16)
    steps = length // TILE

    def exchange(values):
        return lax.all_to_all(values, "space", 0, 0, tiled=True)

    def mix(got, rows, given):
        adjoint = bool(given)
        shape = (mode_rows, 2 * kx_count // samples, LANES)
        block = jax.ShapeDtypeStruct((2,) + shape if adjoint else shape, BF16)
        outs = pl.pallas_call(
            lambda *refs: modes_kernel(*refs, adjoint=adjoint, samples=samples),
            out_shape=[exchange_shape] + [block] * samples,
            in_specs=[pl.BlockSpec(memory_space=pltpu.SMEM)] + [VMEM] * (4 + len(given)),
            out_specs=[VMEM] * (1 + samples),
            scratch_shapes=[
                pltpu.VMEM((lines // LANES, groups * slots, LANES), F32),
                pltpu.VMEM((mode_rows, rows_here * groups, LANES), BF16),
                pltpu.VMEM((mode_rows, 2 * kx_count, LANES), F32),
                pltpu.VMEM((2 * kx_count, LANES), F32),
            ],
            compiler_params=params(10),
            name="adjoint_modes" if adjoint else "mix_modes",
        )(place, got, mode_weight, rows, back_rows, *given)
        return outs[0], outs[1:]

    def share(blocks):
        return [blocks[0]] + [
            lax.ppermute(
                blocks[k], "dp", [(a, (a + k) % samples) for a in range(samples)]
            )
            for k in range(1, samples)
        ]

    columns, near_signal = pl.pallas_call(
        columns_kernel,
        out_shape=[exchange_shape, jax.ShapeDtypeStruct((lines, length), BF16)],
        in_specs=[HBM, HBM],
        out_specs=[VMEM, VMEM],
        scratch_shapes=[
            pltpu.VMEM(table.shape, BF16),
            pltpu.VMEM((2 * ky_count, lines), F32),
            pltpu.SemaphoreType.DMA((2, steps)),
        ],
        compiler_params=params(14),
        name="columns",
    )(pinned(table), pinned(signal))
    columns, place = lax.optimization_barrier((columns, place))
    sent, spectrum = mix(exchange(columns), mix_rows, ())
    back = exchange(sent)
    response, delta, delta_columns = pl.pallas_call(
        field_kernel,
        out_shape=[lines_shape, lines_shape, exchange_shape],
        in_specs=[VMEM, VMEM, VMEM, HBM, VMEM],
        out_specs=[HBM, HBM, VMEM],
        scratch_shapes=[pltpu.VMEM((lines, length), BF16)] * 3
        + [
            pltpu.VMEM((lines, 2 * ky_count), BF16),
            pltpu.VMEM((DIAGONAL, DIAGONAL), BF16),
            pltpu.VMEM((2, lines, TILE), F32),
            pltpu.VMEM((2 * ky_count, lines), F32),
            pltpu.SemaphoreType.DMA((3, steps)),
        ],
        compiler_params=params(20),
        name="field_step",
    )(back, table, near_signal, pinned(upstream), mix_weight)
    sent, both_modes = mix(exchange(delta_columns), adjoint_rows, spectrum)
    shared = share(both_modes)
    back = exchange(sent)
    mode_grad = pl.pallas_call(
        lambda *refs: mode_grad_kernel(*refs, samples=samples),
        out_shape=jax.ShapeDtypeStruct(
            (mode_rows, kx_count // samples, channels, LANES), F32
        ),
        in_specs=[VMEM] * samples,
        out_specs=VMEM,
        compiler_params=params(8),
        name="mode_grad",
    )(*shared)
    field_grad = pl.pallas_call(
        grad_kernel,
        out_shape=lines_shape,
        in_specs=[VMEM, VMEM, HBM, VMEM],
        out_specs=HBM,
        scratch_shapes=[
            pltpu.VMEM((lines, length), BF16),
            pltpu.VMEM((lines, 2 * ky_count), BF16),
            pltpu.VMEM((DIAGONAL, DIAGONAL), BF16),
            pltpu.VMEM((lines, length), BF16),
            pltpu.SemaphoreType.DMA((2, steps)),
        ],
        compiler_params=params(16),
        name="field_grad",
    )(back, table, pinned(delta), mix_weight)
    return (response.reshape(fields.shape), field_grad.reshape(fields.shape), mode_grad)


def solution(mesh):
    in_specs = (
        P("dp", "space", None, None),
        P("dp", "space", None, None),
        P("space", None, None, None),
        P(),
    )
    out_specs = (
        P("dp", "space", None, None),
        P("dp", "space", None, None),
        P("space", "dp", None, None),
    )
    return jax.shard_map(
        on_device, mesh=mesh, in_specs=in_specs, out_specs=out_specs, check_vma=False
    )
```

time: 117 us -> 85.4 us (0.73)
  matrix products: 38.2 us -> 0 us
  Pallas kernels: 0 us -> 29.4 us
  blocking collectives: 18.4 us -> 43.4 us
  waiting for transfers between devices: 26 us -> 2.4 us
  starting transfers between devices: 21.4 us -> 8.6 us
  local copies, waits for them, and re-layouts: 11.5 us -> 0.03 us
    dot_general x16 -> x0, matrix products: 38.2 us -> none  [the longest x1 8.47 us: on_device(): jnp.einsum('rcn,cd->rdn', signal, mix_weight, preferred_element_type=jnp....]
    pallas_call x0 -> x6, Pallas kernels: none -> 29.4 us  [the longest x1 10.7 us: on_device(): pl.pallas_call(field_kernel, out_shape=[lines_shape, lines_shape, exchang...]
    all_to_all x5 -> x1, waiting for transfers between devices: 26 us -> 0.14 us  [exchange(): return lax.all_to_all(values, 'space', 0, 0, tiled=True)]
    all_to_all x1 -> x3, blocking collectives: 18.4 us -> 43.4 us  [exchange(): return lax.all_to_all(values, 'space', 0, 0, tiled=True)]
    all_to_all x5 -> x1, starting transfers between devices: 21.4 us -> 3.71 us  [exchange(): return lax.all_to_all(values, 'space', 0, 0, tiled=True)]
    unnamed x28 -> x12, local copies, waits for them, and re-layouts: 5.1 us -> 0.03 us
    ppermute x0 -> x3, starting transfers between devices: none -> 4.89 us  [share(): lax.ppermute(blocks[k], 'dp', [(a, (a + k) % samples) for a in range(samp...]
    reshape x5 -> x0, local copies, waits for them, and re-layouts: 2.76 us -> none  [the longest x2 2.06 us: to_rows(): sent = back.reshape(groups, 2 * mode_rows, rows_here * channels)]
  transfers between devices with their start and end apart: 5 -> 4, of which waited for: 4 -> 3; matrix products, arithmetic and copies ran while one was open for 15% -> 0% of each run, Pallas kernels for 0% -> 2%
where the time goes in v2:
time: 85.4 us; the launch traced here: 84.8 us
  blocking collectives  43.4 us (51%)
  Pallas kernels  29.4 us (34%)
  starting transfers between devices  8.6 us (10%)
  waiting for transfers between devices  2.4 us (3%)
  between operations  0.9 us (1%)
    all_to_all x3, blocking collectives, exchange(): return lax.all_to_all(values, 'space', 0, 0, tiled=True)  43.4 us
    pallas_call x1, Pallas kernels, on_device(): pl.pallas_call(field_kernel, out_shape=[lines_shape, lines_shape, exchang...  10.7 us
    pallas_call x2, Pallas kernels, mix(): pl.pallas_call(lambda *refs: modes_kernel(*refs, adjoint=adjoint, samples...  6.15 us
    pallas_call x1, Pallas kernels, on_device(): pl.pallas_call(grad_kernel, out_shape=lines_shape, in_specs=[VMEM, VMEM,...  5.53 us
    pallas_call x1, Pallas kernels, on_device(): pl.pallas_call(columns_kernel, out_shape=[exchange_shape, jax.ShapeDtypeS...  5.23 us
    ppermute x3, starting transfers between devices, share(): lax.ppermute(blocks[k], 'dp', [(a, (a + k) % samples) for a in range(samp...  4.89 us
    all_to_all x1, starting transfers between devices, exchange(): return lax.all_to_all(values, 'space', 0, 0, tiled=True)  3.71 us
    ppermute x3, waiting for transfers between devices, share(): lax.ppermute(blocks[k], 'dp', [(a, (a + k) % samples) for a in range(samp...  2.26 us
  transfers between devices with their start and end apart: 4, of which 3 were waited for; matrix products, arithmetic and copies ran while one was open for 0% of the time, Pallas kernels for 2%

profile of v2, /device:TPU:1, one launch (start us, length us, event | category | flops | bytes accessed | tf_op | source)
XLA Modules:
  0.0 84.8 jit_solution(2326989274136256841)
XLA Ops:
  0.6 0.0 copy-start.2
  0.6 0.0 copy-start.4
  0.7 0.0 copy-start.1
  0.7 5.2 %columns.1 = (bf16[32,8,512]{2,1,0:T(8,128)(2,1)S(1)}, bf16[512,4096]{1,0:T(8,128)(2,1)S(1)}) custom-call(bf16[256,4096]{1,0:T(8,128)(2,1)} %constant.14.clone.table_hbm.table_ref, bf16[512,4096]{1,0:T(8,128)(2,1)} %bitcast.5), custom_call_target="tpu_custom_call" | custom-call | tf_op jit(solution)/shard_map/columns/pallas_call | solution.py:400
  5.9 0.0 copy-start
  5.9 0.0 copy-start.5
  5.9 18.5 %all_to_all.20.refs_1_ = bf16[32,8,512]{2,1,0:T(8,128)(2,1)S(1)} all-to-all(bf16[32,8,512]{2,1,0:T(8,128)(2,1)S(1)} %get-tuple-element.22), channel_id=1, replica_groups=mesh['dp'=4,'space'=32] {'space'}, dimensions={0} | all-to-all | bytes 524288 | tf_op jit(solution)/shard_map/all_to_all | solution.py:370
  24.5 0.0 copy-done.2
  24.5 0.0 copy-done.4
  24.5 2.4 %mix_modes.1 = (bf16[32,8,512]{2,1,0:T(8,128)(2,1)S(1)}, bf16[4,32,128]{2,1,0:T(8,128)(2,1)S(1)}, bf16[4,32,128]{2,1,0:T(8,128)(2,1)S(1)}, bf16[4,32,128]{2,1,0:T(8,128)(2,1)S(1)}, bf16[4,32,128]{2,1,0:T(8,128)(2,1)S(1)}) custom-call(s32[1]{0:T(128)} %bitcast.1.refs_0_, bf16[32,8,512]{2,1,0:T(8,128)(2,1)S(1)} %all_to_all.20.refs_1_, ...), custom_call_target="tpu_custom_call" | custom-call | tf_op jit(solution)/shard_map/mix_modes/pallas_call | solution.py:376
  26.9 12.4 %all_to_all.21.back_ref = bf16[32,8,512]{2,1,0:T(8,128)(2,1)S(1)} all-to-all(bf16[32,8,512]{2,1,0:T(8,128)(2,1)S(1)} %get-tuple-element.23), channel_id=1, replica_groups=mesh['dp'=4,'space'=32] {'space'}, dimensions={0} | all-to-all | bytes 524288 | tf_op jit(solution)/shard_map/all_to_all | solution.py:370
  39.4 10.7 %field_step.1 = (bf16[512,4096]{1,0:T(8,128)(2,1)}, bf16[512,4096]{1,0:T(8,128)(2,1)}, bf16[32,8,512]{2,1,0:T(8,128)(2,1)S(1)}) custom-call(bf16[32,8,512]{2,1,0:T(8,128)(2,1)S(1)} %all_to_all.21.back_ref, bf16[256,4096]{1,0:T(8,128)(2,1)S(1)} %copy-done, bf16[512,4096]{1,0:T(8,128)(2,1)S(1)} %get-tuple-element.24.fields_ref, bf16[512,4096]{1,0:T(8,128)(2,1)} %bitcast.6, ...), custom_call_target="tpu_custom_call" | custom-call | tf_op jit(solution)/shard_map/field_step/pallas_call | solution.py:416
  50.0 12.5 %all_to_all.22.refs_1_ = bf16[32,8,512]{2,1,0:T(8,128)(2,1)S(1)} all-to-all(bf16[32,8,512]{2,1,0:T(8,128)(2,1)S(1)} %get-tuple-element.26), channel_id=1, replica_groups=mesh['dp'=4,'space'=32] {'space'}, dimensions={0} | all-to-all | bytes 524288 | tf_op jit(solution)/shard_map/all_to_all | solution.py:370
  62.5 3.7 %adjoint_modes.1 = (bf16[32,8,512]{2,1,0:T(8,128)(2,1)}, bf16[2,4,32,128]{3,2,1,0:T(8,128)(2,1)S(1)}, bf16[2,4,32,128]{3,2,1,0:T(8,128)(2,1)S(1)}, bf16[2,4,32,1...) custom-call(s32[1]{0:T(128)} %bitcast.1.refs_0_, bf16[32,8,512]{2,1,0:T(8,128)(2,1)S(1)} %all_to_all.22.refs_1_, ...), custom_call_target="tpu_custom_call" | custom-call | tf_op jit(solution)/shard_map/adjoint_modes/pallas_call | solution.py:376
  66.2 3.7 %all-to-all-start.3 = ((bf16[32,8,512]{2,1,0:T(8,128)(2,1)}), bf16[32,8,512]{2,1,0:T(8,128)(2,1)S(1)}, u32[]{:S(2)}, u32[]{:S(2)}) async-start(bf16[32,8,512]{2,1,0:T(8,128)(2,1)} %get-tuple-element.31), calls=%async_computation.3 | async-start | bytes 524288 | tf_op jit(solution)/shard_map/all_to_all | solution.py:370
  69.9 1.3 %collective-permute-start = (bf16[2,4,32,128]{3,2,1,0:T(8,128)(2,1)S(1)}, bf16[2,4,32,128]{3,2,1,0:T(8,128)(2,1)S(1)}, u32[]{:S(2)}, u32[]{:S(2)}) collective-permute-start(bf16[2,4,32,128]{3,2,1,0:T(8,128)(2,1)S(1)} %get-tuple-element.34), channel_id=1, source_target_pairs={{0,32},{32,64},{64,96},{96,0},{1,33},{33,65},{65,97},{97,1},{2,34}... | collective-permute-start | bytes 196616 | tf_op jit(solution)/shard_map/ppermute | solution.py:394
  71.2 2.5 %collective-permute-start.1 = (bf16[2,4,32,128]{3,2,1,0:T(8,128)(2,1)S(1)}, bf16[2,4,32,128]{3,2,1,0:T(8,128)(2,1)S(1)}, u32[]{:S(2)}, u32[]{:S(2)}) collective-permute-start(bf16[2,4,32,128]{3,2,1,0:T(8,128)(2,1)S(1)} %get-tuple-element.35), channel_id=1, source_target_pairs={{0,64},{32,96},{64,0},{96,32},{1,65},{33,97},{65,1},{97,33},{2,66}... | collective-permute-start | bytes 196616 | tf_op jit(solution)/shard_map/ppermute | solution.py:394
  73.7 1.1 %collective-permute-start.2 = (bf16[2,4,32,128]{3,2,1,0:T(8,128)(2,1)S(1)}, bf16[2,4,32,128]{3,2,1,0:T(8,128)(2,1)S(1)}, u32[]{:S(2)}, u32[]{:S(2)}) collective-permute-start(bf16[2,4,32,128]{3,2,1,0:T(8,128)(2,1)S(1)} %get-tuple-element.36), channel_id=1, source_target_pairs={{0,96},{32,0},{64,32},{96,64},{1,97},{33,1},{65,33},{97,65},{2,98}... | collective-permute-start | bytes 196616 | tf_op jit(solution)/shard_map/ppermute | solution.py:394
  74.8 0.0 collective-permute-done.refs_1_
  74.8 2.1 %collective-permute-done.1.refs_2_ = bf16[2,4,32,128]{3,2,1,0:T(8,128)(2,1)S(1)} collective-permute-done((bf16[2,4,32,128]{3,2,1,0:T(8,128)(2,1)S(1)}, bf16[2,4,32,128]{3,2,1,0:T(8,128)(2,1)S(1)}, u32[]{:S(2)}, u32[]{:S(2)}) %collective-permute-start.1) | collective-permute-done | bytes 65568 | tf_op jit(solution)/shard_map/ppermute | solution.py:394
  77.0 0.1 collective-permute-done.2.refs_3_
  77.1 1.8 %mode_grad.1 = f32[4,16,64,128]{3,2,1,0:T(8,128)} custom-call(bf16[2,4,32,128]{3,2,1,0:T(8,128)(2,1)S(1)} %get-tuple-element.33.refs_0_, bf16[2,4,32,128]{3,2,1,0:T(8,128)(2,1)S(1)} %collective-permute-done.refs_1_, bf16[2,4,32,128]{3,2,1,0:T(8,128)(2,1)S(1)} %collective-permute-done.1.refs_2_, bf16[2,4,32,128]{3,2,1,0:T(8,128)(2,1)S(1)} %collective-permute-done.2.refs_3_), custom_call_target="tpu_custom_call" | custom-call | tf_op jit(solution)/shard_map/mode_grad/pallas_call | solution.py:435
  78.9 0.1 all-to-all-done.3.back_ref
  79.0 5.5 %field_grad.1 = bf16[512,4096]{1,0:T(8,128)(2,1)} custom-call(bf16[32,8,512]{2,1,0:T(8,128)(2,1)S(1)} %all-to-all-done.3.back_ref, bf16[256,4096]{1,0:T(8,128)(2,1)S(1)} %copy-done, bf16[512,4096]{1,0:T(8,128)(2,1)} %get-tuple-element.32.delta_hbm, bf16[64,64]{1,0:T(8,128)(2,1)S(1)} %copy-done.5), custom_call_target="tpu_custom_call" | custom-call | tf_op jit(solution)/shard_map/field_grad/pallas_call | solution.py:445
  (5 shorter events, 0.0 us)
Async XLA Ops:
  0.6 23.8 %copy-start.2 = (bf16[2,256,128]{2,1,0:T(8,128)(2,1)S(1)}, bf16[2,256,128]{2,1,0:T(8,128)(2,1)}, u32[]{:S(2)}) copy-start(bf16[2,256,128]{2,1,0:T(8,128)(2,1)} %constant.17.clone.refs_4_) | copy-start | bytes 393220
  0.6 23.8 %copy-start.4 = (bf16[2,256,256]{2,1,0:T(8,128)(2,1)S(1)}, bf16[2,256,256]{2,1,0:T(8,128)(2,1)}, u32[]{:S(2)}) copy-start(bf16[2,256,256]{2,1,0:T(8,128)(2,1)} %constant.15.clone.refs_3_) | copy-start | bytes 786436
  0.7 23.8 %copy-start.1 = (bf16[4,64,64,128]{3,2,1,0:T(8,128)(2,1)S(1)}, bf16[4,64,64,128]{3,2,1,0:T(8,128)(2,1)}, u32[]{:S(2)}) copy-start(bf16[4,64,64,128]{3,2,1,0:T(8,128)(2,1)} %refs_2_.3) | copy-start | bytes 12582916
  5.9 33.4 %copy-start = (bf16[256,4096]{1,0:T(8,128)(2,1)S(1)}, bf16[256,4096]{1,0:T(8,128)(2,1)}, u32[]{:S(2)}) copy-start(bf16[256,4096]{1,0:T(8,128)(2,1)} %constant.14.clone.table_hbm.table_ref) | copy-start | bytes 6291460
  5.9 33.4 %copy-start.5 = (bf16[64,64]{1,0:T(8,128)(2,1)S(1)}, bf16[64,64]{1,0:T(8,128)(2,1)}, u32[]{:S(2)}) copy-start(bf16[64,64]{1,0:T(8,128)(2,1)} %weight_ref.3) | copy-start | bytes 24580
  39.4 23.1 %copy-start.3 = (bf16[2,256,256]{2,1,0:T(8,128)(2,1)S(1)}, bf16[2,256,256]{2,1,0:T(8,128)(2,1)}, u32[]{:S(2)}) copy-start(bf16[2,256,256]{2,1,0:T(8,128)(2,1)} %constant.16.clone.refs_3_) | copy-start | bytes 786436
  66.2 12.8 %all-to-all-start.3 = ((bf16[32,8,512]{2,1,0:T(8,128)(2,1)}), bf16[32,8,512]{2,1,0:T(8,128)(2,1)S(1)}, u32[]{:S(2)}, u32[]{:S(2)}) async-start(bf16[32,8,512]{2,1,0:T(8,128)(2,1)} %get-tuple-element.31), calls=%async_computation.3 | async-start | bytes 524288 | tf_op jit(solution)/shard_map/all_to_all | solution.py:370
  69.9 4.9 %collective-permute-start = (bf16[2,4,32,128]{3,2,1,0:T(8,128)(2,1)S(1)}, bf16[2,4,32,128]{3,2,1,0:T(8,128)(2,1)S(1)}, u32[]{:S(2)}, u32[]{:S(2)}) collective-permute-start(bf16[2,4,32,128]{3,2,1,0:T(8,128)(2,1)S(1)} %get-tuple-element.34), channel_id=1, source_target_pairs={{0,32},{32,64},{64,96},{96,0},{1,33},{33,65},{65,97},{97,1},{2,34}... | collective-permute-start | bytes 196616 | tf_op jit(solution)/shard_map/ppermute | solution.py:394
  71.2 5.7 %collective-permute-start.1 = (bf16[2,4,32,128]{3,2,1,0:T(8,128)(2,1)S(1)}, bf16[2,4,32,128]{3,2,1,0:T(8,128)(2,1)S(1)}, u32[]{:S(2)}, u32[]{:S(2)}) collective-permute-start(bf16[2,4,32,128]{3,2,1,0:T(8,128)(2,1)S(1)} %get-tuple-element.35), channel_id=1, source_target_pairs={{0,64},{32,96},{64,0},{96,32},{1,65},{33,97},{65,1},{97,33},{2,66}... | collective-permute-start | bytes 196616 | tf_op jit(solution)/shard_map/ppermute | solution.py:394
  73.7 3.4 %collective-permute-start.2 = (bf16[2,4,32,128]{3,2,1,0:T(8,128)(2,1)S(1)}, bf16[2,4,32,128]{3,2,1,0:T(8,128)(2,1)S(1)}, u32[]{:S(2)}, u32[]{:S(2)}) collective-permute-start(bf16[2,4,32,128]{3,2,1,0:T(8,128)(2,1)S(1)} %get-tuple-element.36), channel_id=1, source_target_pairs={{0,96},{32,0},{64,32},{96,64},{1,97},{33,1},{65,33},{97,65},{2,98}... | collective-permute-start | bytes 196616 | tf_op jit(solution)/shard_map/ppermute | solution.py:394

commit v3 on v2

--- a/solution.py
+++ b/solution.py
@@ -16,7 +16,8 @@
 STACK = 4
 TILE = 512
 DIAGONAL = 256
-AHEAD = 3
+LOAD_TILE = 1024
+AHEAD = 4
 MIB = 1024 * 1024
 
 
@@ -75,21 +76,20 @@
     return jnp.where((row == 0) | (row == mode_rows), values, values * 2.0)
 
 
-def tiles(length):
-    return [slice(at, at + TILE) for at in range(0, length, TILE)]
+def tiles(length, size):
+    return [slice(at, at + size) for at in range(0, length, size)]
 
 
 class Loads:
-    def __init__(self, pairs, sem_ref, ahead):
+    def __init__(self, pairs, sem_ref, size):
         self.copies = [
             [
                 pltpu.make_async_copy(source.at[:, cols], target.at[:, cols], sem_ref.at[n, k])
                 for n, (source, target) in enumerate(pairs)
             ]
-            for k, cols in enumerate(tiles(pairs[0][0].shape[1]))
+            for k, cols in enumerate(tiles(pairs[0][0].shape[1], size))
         ]
-        self.ahead = ahead
-        for k in range(ahead):
+        for k in range(AHEAD):
             self.start(k)
 
     def start(self, k):
@@ -100,12 +100,16 @@
     def wait(self, k):
         for copy in self.copies[k]:
             copy.wait()
-        self.start(k + self.ahead)
-
-
-def columns_kernel(table_hbm, fields_hbm, out_ref, fields_ref, table_ref, acc_ref, sem_ref):
-    parts = tiles(table_hbm.shape[1])
-    loads = Loads(((table_hbm, table_ref), (fields_hbm, fields_ref)), sem_ref, AHEAD)
+        self.start(k + AHEAD)
+
+
+def columns_kernel(
+    table_hbm, fields_hbm, upstream_hbm, weight_hbm,
+    out_ref, fields_ref, table_ref, acc_ref, sem_ref,
+):
+    del upstream_hbm, weight_hbm
+    parts = tiles(table_hbm.shape[1], LOAD_TILE)
+    loads = Loads(((table_hbm, table_ref), (fields_hbm, fields_ref)), sem_ref, LOAD_TILE)
     for k, cols in enumerate(parts):
         loads.wait(k)
         product = dot_nt(table_ref[:, cols], fields_ref[:, cols])
@@ -220,45 +224,51 @@
         out_ref[at : at + size, at : at + size] = block
 
 
+def gelu_chunk(pre_ref, upstream_ref, response_ref, delta_ref, slot, rows, cols):
+    v = pre_ref[slot, rows, :]
+    t = jnp.tanh(v * (GELU_SCALE + (GELU_SCALE * GELU_CUBIC) * (v * v)))
+    half = (0.5 + 0.5 * t).astype(BF16)
+    rest = (1.0 - t * t).astype(BF16)
+    v = v.astype(BF16)
+    response_ref[rows, cols] = v * half
+    inner = (0.5 * GELU_SCALE) + (1.5 * GELU_SCALE * GELU_CUBIC) * (v * v)
+    delta_ref[rows, cols] = upstream_ref[rows, cols] * (half + v * rest * inner)
+
+
 def field_kernel(
-    back_ref, table_ref, fields_ref, upstream_hbm, weight_ref,
+    back_ref, table_ref, fields_ref, upstream_ref, weight_ref,
     response_hbm, delta_hbm, sent_ref,
-    upstream_ref, response_ref, delta_ref, turned_ref, mix_ref, pre_ref, acc_ref, sem_ref,
+    response_ref, delta_ref, turned_ref, mix_ref, pre_ref, acc_ref, sem_ref,
 ):
-    loads = Loads(((upstream_hbm, upstream_ref),), sem_ref, AHEAD)
     mode_rows = back_ref.shape[1] // 2
     turned_ref[...] = transposed_back(back_ref, mode_rows, True)
     spread(weight_ref[...].astype(F32).T.astype(BF16), mix_ref)
     width = mix_ref.shape[0]
     total = fields_ref.shape[0]
     chunk = 32
-    parts = tiles(table_ref.shape[1])
+    parts = tiles(table_ref.shape[1], TILE)
     copies = []
+
+    def preact(k, at):
+        rows = slice(at, at + width)
+        pre_ref[k % 2, rows, :] = dot_nn(turned_ref[rows, :], table_ref[:, parts[k]]) + dot_nn(
+            mix_ref[...], fields_ref[rows, parts[k]]
+        )
+
+    for at in range(0, total, width):
+        preact(0, at)
     for k, cols in enumerate(parts):
-        slot = k % pre_ref.shape[0]
-        for at in range(0, total, width):
-            rows = slice(at, at + width)
-            pre_ref[slot, rows, :] = dot_nn(turned_ref[rows, :], table_ref[:, cols]) + dot_nn(
-                mix_ref[...], fields_ref[rows, cols]
-            )
-        loads.wait(k)
         for at in range(0, total, chunk):
+            if at % width == 0 and k + 1 < len(parts):
+                preact(k + 1, at)
             rows = slice(at, at + chunk)
-            v = pre_ref[slot, rows, :]
-            square = v * v
-            half = 0.5 + 0.5 * jnp.tanh(v * (GELU_SCALE + (GELU_SCALE * GELU_CUBIC) * square))
-            value = v * half
-            response_ref[rows, cols] = value.astype(BF16)
-            slope = half + value * (1.0 - half) * (
-                2.0 * GELU_SCALE + (6.0 * GELU_SCALE * GELU_CUBIC) * square
-            )
-            delta_ref[rows, cols] = (upstream_ref[rows, cols].astype(F32) * slope).astype(BF16)
+            gelu_chunk(pre_ref, upstream_ref, response_ref, delta_ref, k % 2, rows, cols)
         for n, (source, target) in enumerate(
             ((response_ref, response_hbm), (delta_ref, delta_hbm))
         ):
             copies.append(
                 pltpu.make_async_copy(
-                    source.at[:, cols], target.at[:, cols], sem_ref.at[1 + n, k]
+                    source.at[:, cols], target.at[:, cols], sem_ref.at[n, k]
                 )
             )
             copies[-1].start()
@@ -274,16 +284,34 @@
         copy.wait()
 
 
-def grad_kernel(
-    back_ref, table_ref, delta_hbm, weight_ref, out_hbm,
-    delta_ref, turned_ref, mix_ref, out_ref, sem_ref,
-):
-    loads = Loads(((delta_hbm, delta_ref),), sem_ref, AHEAD)
+def mode_products(shared_refs, out_ref, i):
+    _, kx_here, channels, _ = out_ref.shape
+    stack_rows = 2 * STACK
+    count = len(shared_refs) * stack_rows
+    row = lax.broadcasted_iota(jnp.int32, (count, LANES), 0) % stack_rows // 2
+    for g in range(kx_here // STACK):
+        rows = slice(g * stack_rows, (g + 1) * stack_rows)
+        x = jnp.concatenate([ref[0, i, rows, :].astype(F32) for ref in shared_refs], axis=0)
+        d = jnp.concatenate([ref[1, i, rows, :].astype(F32) for ref in shared_refs], axis=0)
+        wide = jnp.concatenate([jnp.where(row == m, d, 0.0) for m in range(STACK)], axis=1)
+        product = dot_nn(x.T[:channels].astype(BF16), wide.astype(BF16))
+        for m in range(STACK):
+            out_ref[i, g * STACK + m] = product[:, m * LANES : (m + 1) * LANES]
+
+
+def grad_kernel(back_ref, table_ref, delta_hbm, weight_ref, *rest, samples):
+    shared_refs, (out_hbm, modes_hbm) = rest[:samples], rest[samples : samples + 2]
+    delta_ref, turned_ref, mix_ref, out_ref, modes_ref, sem_ref = rest[samples + 2 :]
+    loads = Loads(((delta_hbm, delta_ref),), sem_ref, LOAD_TILE)
     turned_ref[...] = transposed_back(back_ref, 0, False)
     spread(weight_ref[...], mix_ref)
     width = mix_ref.shape[0]
     copies = []
-    for k, cols in enumerate(tiles(table_ref.shape[1])):
+    for i in range(modes_ref.shape[0]):
+        mode_products(shared_refs, modes_ref, i)
+        copies.append(pltpu.make_async_copy(modes_ref.at[i], modes_hbm.at[i], sem_ref.at[2, i]))
+        copies[-1].start()
+    for k, cols in enumerate(tiles(table_ref.shape[1], LOAD_TILE)):
         loads.wait(k)
         for at in range(0, delta_ref.shape[0], width):
             rows = slice(at, at + width)
@@ -291,39 +319,24 @@
                 dot_nn(turned_ref[rows, :], table_ref[:, cols])
                 + dot_nn(mix_ref[...], delta_ref[rows, cols])
             ).astype(BF16)
-        copy = pltpu.make_async_copy(out_ref.at[:, cols], out_hbm.at[:, cols], sem_ref.at[1, k])
-        copy.start()
-        copies.append(copy)
+        copies.append(
+            pltpu.make_async_copy(out_ref.at[:, cols], out_hbm.at[:, cols], sem_ref.at[1, k])
+        )
+        copies[-1].start()
     for copy in copies:
         copy.wait()
 
 
-def mode_grad_kernel(*refs, samples):
-    shared_refs, out_ref = refs[:samples], refs[samples]
-    mode_rows, kx_here, channels, _ = out_ref.shape
-    stack_rows = 2 * STACK
-    count = samples * stack_rows
-    row = lax.broadcasted_iota(jnp.int32, (count, LANES), 0) % stack_rows // 2
-    for i in range(mode_rows):
-        for g in range(kx_here // STACK):
-            rows = slice(g * stack_rows, (g + 1) * stack_rows)
-            x = jnp.concatenate([ref[0, i, rows, :].astype(F32) for ref in shared_refs], axis=0)
-            d = jnp.concatenate([ref[1, i, rows, :].astype(F32) for ref in shared_refs], axis=0)
-            wide = jnp.concatenate(
-                [jnp.where(row == m, d, 0.0) for m in range(STACK)], axis=1
-            ).astype(BF16)
-            turned = x.T[:channels].astype(BF16)
-            product = dot_nn(turned, wide)
-            for m in range(STACK):
-                out_ref[i, g * STACK + m] = product[:, m * LANES : (m + 1) * LANES]
-
-
 VMEM = pl.BlockSpec(memory_space=pltpu.VMEM)
 HBM = pl.BlockSpec(memory_space=pltpu.HBM)
 
 
 def pinned(values):
     return pltpu.with_memory_space_constraint(values, pltpu.HBM)
+
+
+def cost(mib):
+    return pl.CostEstimate(flops=0, transcendentals=0, bytes_accessed=mib * MIB)
 
 
 def params(mib):
@@ -385,6 +398,7 @@
                 pltpu.VMEM((2 * kx_count, LANES), F32),
             ],
             compiler_params=params(10),
+            cost_estimate=cost(16),
             name="adjoint_modes" if adjoint else "mix_modes",
         )(place, got, mode_weight, rows, back_rows, *given)
         return outs[0], outs[1:]
@@ -400,63 +414,58 @@
     columns, near_signal = pl.pallas_call(
         columns_kernel,
         out_shape=[exchange_shape, jax.ShapeDtypeStruct((lines, length), BF16)],
-        in_specs=[HBM, HBM],
+        in_specs=[HBM] * 4,
         out_specs=[VMEM, VMEM],
         scratch_shapes=[
             pltpu.VMEM(table.shape, BF16),
             pltpu.VMEM((2 * ky_count, lines), F32),
-            pltpu.SemaphoreType.DMA((2, steps)),
+            pltpu.SemaphoreType.DMA((2, length // LOAD_TILE)),
         ],
         compiler_params=params(14),
+        cost_estimate=cost(16),
         name="columns",
-    )(pinned(table), pinned(signal))
+    )(pinned(table), pinned(signal), pinned(upstream), pinned(mode_weight))
     columns, place = lax.optimization_barrier((columns, place))
     sent, spectrum = mix(exchange(columns), mix_rows, ())
     back = exchange(sent)
     response, delta, delta_columns = pl.pallas_call(
         field_kernel,
         out_shape=[lines_shape, lines_shape, exchange_shape],
-        in_specs=[VMEM, VMEM, VMEM, HBM, VMEM],
+        in_specs=[VMEM] * 5,
         out_specs=[HBM, HBM, VMEM],
-        scratch_shapes=[pltpu.VMEM((lines, length), BF16)] * 3
+        scratch_shapes=[pltpu.VMEM((lines, length), BF16)] * 2
         + [
             pltpu.VMEM((lines, 2 * ky_count), BF16),
             pltpu.VMEM((DIAGONAL, DIAGONAL), BF16),
             pltpu.VMEM((2, lines, TILE), F32),
             pltpu.VMEM((2 * ky_count, lines), F32),
-            pltpu.SemaphoreType.DMA((3, steps)),
+            pltpu.SemaphoreType.DMA((2, steps)),
         ],
         compiler_params=params(20),
+        cost_estimate=cost(24),
         name="field_step",
-    )(back, table, near_signal, pinned(upstream), mix_weight)
+    )(back, table, near_signal, upstream, mix_weight)
     sent, both_modes = mix(exchange(delta_columns), adjoint_rows, spectrum)
     shared = share(both_modes)
     back = exchange(sent)
-    mode_grad = pl.pallas_call(
-        lambda *refs: mode_grad_kernel(*refs, samples=samples),
-        out_shape=jax.ShapeDtypeStruct(
-            (mode_rows, kx_count // samples, channels, LANES), F32
-        ),
-        in_specs=[VMEM] * samples,
-        out_specs=VMEM,
-        compiler_params=params(8),
-        name="mode_grad",
-    )(*shared)
-    field_grad = pl.pallas_call(
-        grad_kernel,
-        out_shape=lines_shape,
-        in_specs=[VMEM, VMEM, HBM, VMEM],
-        out_specs=HBM,
+    modes_shape = pltpu.HBM((mode_rows, kx_count // samples, channels, LANES), F32)
+    field_grad, mode_grad = pl.pallas_call(
+        lambda *refs: grad_kernel(*refs, samples=samples),
+        out_shape=[lines_shape, modes_shape],
+        in_specs=[VMEM, VMEM, HBM, VMEM] + [VMEM] * samples,
+        out_specs=[HBM, HBM],
         scratch_shapes=[
             pltpu.VMEM((lines, length), BF16),
             pltpu.VMEM((lines, 2 * ky_count), BF16),
             pltpu.VMEM((DIAGONAL, DIAGONAL), BF16),
             pltpu.VMEM((lines, length), BF16),
-            pltpu.SemaphoreType.DMA((2, steps)),
+            pltpu.VMEM(modes_shape.shape, F32),
+            pltpu.SemaphoreType.DMA((3, max(length // LOAD_TILE, mode_rows))),
         ],
-        compiler_params=params(16),
-        name="field_grad",
-    )(back, table, pinned(delta), mix_weight)
+        compiler_params=params(20),
+        cost_estimate=cost(16),
+        name="gradients",
+    )(back, table, pinned(delta), mix_weight, *shared)
     return (response.reshape(fields.shape), field_grad.reshape(fields.shape), mode_grad)
 
 

time: 85.4 us -> 80.8 us (0.946)
  Pallas kernels: 29.4 us -> 23 us
  waiting for transfers between devices: 2.4 us -> 4.22 us
    pallas_call x1, Pallas kernels: 10.7 us -> 7.8 us  [on_device(): pl.pallas_call(field_kernel, out_shape=[lines_shape, lines_shape, exchang...]
    pallas_call x2 -> x1, Pallas kernels: 7.34 us -> 5.53 us  [on_device(): pl.pallas_call(lambda *refs: grad_kernel(*refs, samples=samples), out_sha...]
    all_to_all x1, waiting for transfers between devices: 0.14 us -> 1.95 us  [exchange(): return lax.all_to_all(values, 'space', 0, 0, tiled=True)]
    pallas_call x1, Pallas kernels: 5.23 us -> 3.52 us  [on_device(): pl.pallas_call(columns_kernel, out_shape=[exchange_shape, jax.ShapeDtypeS...]
  transfers between devices with their start and end apart: 4 -> 4, of which waited for: 3 -> 3; matrix products, arithmetic and copies ran while one was open for 0% -> 0% of each run, Pallas kernels for 2% -> 0%
where the time goes in v3:
time: 80.8 us; the launch traced here: 80.5 us
  blocking collectives  43.6 us (54%)
  Pallas kernels  23 us (28%)
  starting transfers between devices  8.78 us (11%)
  waiting for transfers between devices  4.22 us (5%)
  between operations  0.9 us (1%)
    all_to_all x3, blocking collectives, exchange(): return lax.all_to_all(values, 'space', 0, 0, tiled=True)  43.6 us
    pallas_call x1, Pallas kernels, on_device(): pl.pallas_call(field_kernel, out_shape=[lines_shape, lines_shape, exchang...  7.8 us
    pallas_call x2, Pallas kernels, mix(): pl.pallas_call(lambda *refs: modes_kernel(*refs, adjoint=adjoint, samples...  6.15 us
    pallas_call x1, Pallas kernels, on_device(): pl.pallas_call(lambda *refs: grad_kernel(*refs, samples=samples), out_sha...  5.53 us
    ppermute x3, starting transfers between devices, share(): lax.ppermute(blocks[k], 'dp', [(a, (a + k) % samples) for a in range(samp...  4.88 us
    all_to_all x1, starting transfers between devices, exchange(): return lax.all_to_all(values, 'space', 0, 0, tiled=True)  3.9 us
    pallas_call x1, Pallas kernels, on_device(): pl.pallas_call(columns_kernel, out_shape=[exchange_shape, jax.ShapeDtypeS...  3.52 us
    ppermute x3, waiting for transfers between devices, share(): lax.ppermute(blocks[k], 'dp', [(a, (a + k) % samples) for a in range(samp...  2.27 us
  transfers between devices with their start and end apart: 4, of which 3 were waited for; matrix products, arithmetic and copies ran while one was open for 0% of the time, Pallas kernels for 0%

profile of v3, /device:TPU:1, one launch (start us, length us, event | category | flops | bytes accessed | tf_op | source)
XLA Modules:
  0.0 80.5 jit_solution(5319643409571222594)
XLA Ops:
  0.6 0.0 copy-start.3
  0.7 0.0 copy-start.5
  0.7 3.5 %columns.1 = (bf16[32,8,512]{2,1,0:T(8,128)(2,1)S(1)}, bf16[512,4096]{1,0:T(8,128)(2,1)S(1)}) custom-call(bf16[256,4096]{1,0:T(8,128)(2,1)} %constant.14.clone.table_hbm.table_ref.refs_1_, bf16[512,4096]{1,0:T(8,128)(2,1)} %bitcast.7, bf16[512,4096]{1,0:T(8,128)(2,1)} %bitcast.5, bf16[4,64,64,128]{3,2,1,0:T(8,128)(2,1)} %refs_2_.3), custom_call_target="tpu_custom_call" | custom-call | bytes 16777216 | tf_op jit(solution)/shard_map/columns/pallas_call | solution.py:414
  4.2 0.0 copy-start.1
  4.2 0.0 copy-start.6
  4.2 18.7 %all_to_all.20.refs_1_ = bf16[32,8,512]{2,1,0:T(8,128)(2,1)S(1)} all-to-all(bf16[32,8,512]{2,1,0:T(8,128)(2,1)S(1)} %get-tuple-element.24), channel_id=1, replica_groups=mesh['dp'=4,'space'=32] {'space'}, dimensions={0} | all-to-all | bytes 524288 | tf_op jit(solution)/shard_map/all_to_all | solution.py:383
  22.9 0.0 copy-done.3
  22.9 2.4 %mix_modes.1 = (bf16[32,8,512]{2,1,0:T(8,128)(2,1)S(1)}, bf16[4,32,128]{2,1,0:T(8,128)(2,1)S(1)}, bf16[4,32,128]{2,1,0:T(8,128)(2,1)S(1)}, bf16[4,32,128]{2,1,0:T(8,128)(2,1)S(1)}, bf16[4,32,128]{2,1,0:T(8,128)(2,1)S(1)}) custom-call(s32[1]{0:T(128)} %bitcast.2.refs_0_, bf16[32,8,512]{2,1,0:T(8,128)(2,1)S(1)} %all_to_all.20.refs_1_, ...), custom_call_target="tpu_custom_call" | custom-call | bytes 16777216 | tf_op jit(solution)/shard_map/mix_modes/pallas_call | solution.py:389
  25.3 12.4 %all_to_all.21.back_ref = bf16[32,8,512]{2,1,0:T(8,128)(2,1)S(1)} all-to-all(bf16[32,8,512]{2,1,0:T(8,128)(2,1)S(1)} %get-tuple-element.25), channel_id=1, replica_groups=mesh['dp'=4,'space'=32] {'space'}, dimensions={0} | all-to-all | bytes 524288 | tf_op jit(solution)/shard_map/all_to_all | solution.py:383
  37.8 0.0 copy-done.1
  37.8 0.0 copy-start.4
  37.8 7.8 %field_step.1 = (bf16[512,4096]{1,0:T(8,128)(2,1)}, bf16[512,4096]{1,0:T(8,128)(2,1)}, bf16[32,8,512]{2,1,0:T(8,128)(2,1)S(1)}) custom-call(bf16[32,8,512]{2,1,0:T(8,128)(2,1)S(1)} %all_to_all.21.back_ref, bf16[256,4096]{1,0:T(8,128)(2,1)S(1)} %copy-done.1, bf16[512,4096]{1,0:T(8,128)(2,1)S(1)} %get-tuple-element.26.fields_ref, ...), custom_call_target="tpu_custom_call" | custom-call | bytes 25165824 | tf_op jit(solution)/shard_map/field_step/pallas_call | solution.py:431
  45.6 12.4 %all_to_all.22.refs_1_ = bf16[32,8,512]{2,1,0:T(8,128)(2,1)S(1)} all-to-all(bf16[32,8,512]{2,1,0:T(8,128)(2,1)S(1)} %get-tuple-element.28), channel_id=1, replica_groups=mesh['dp'=4,'space'=32] {'space'}, dimensions={0} | all-to-all | bytes 524288 | tf_op jit(solution)/shard_map/all_to_all | solution.py:383
  58.1 0.0 copy-done.4
  58.1 3.7 %adjoint_modes.1 = (bf16[32,8,512]{2,1,0:T(8,128)(2,1)}, bf16[2,4,32,128]{3,2,1,0:T(8,128)(2,1)S(1)}, bf16[2,4,32,128]{3,2,1,0:T(8,128)(2,1)S(1)}, bf16[2,4,32,1...) custom-call(s32[1]{0:T(128)} %bitcast.2.refs_0_, bf16[32,8,512]{2,1,0:T(8,128)(2,1)S(1)} %all_to_all.22.refs_1_, ...), custom_call_target="tpu_custom_call" | custom-call | bytes 16777216 | tf_op jit(solution)/shard_map/adjoint_modes/pallas_call | solution.py:389
  61.8 3.9 %all-to-all-start.3 = ((bf16[32,8,512]{2,1,0:T(8,128)(2,1)}), bf16[32,8,512]{2,1,0:T(8,128)(2,1)S(1)}, u32[]{:S(2)}, u32[]{:S(2)}) async-start(bf16[32,8,512]{2,1,0:T(8,128)(2,1)} %get-tuple-element.33), calls=%async_computation.3 | async-start | bytes 524288 | tf_op jit(solution)/shard_map/all_to_all | solution.py:383
  65.7 1.3 %collective-permute-start = (bf16[2,4,32,128]{3,2,1,0:T(8,128)(2,1)S(1)}, bf16[2,4,32,128]{3,2,1,0:T(8,128)(2,1)S(1)}, u32[]{:S(2)}, u32[]{:S(2)}) collective-permute-start(bf16[2,4,32,128]{3,2,1,0:T(8,128)(2,1)S(1)} %get-tuple-element.36), channel_id=1, source_target_pairs={{0,32},{32,64},{64,96},{96,0},{1,33},{33,65},{65,97},{97,1},{2,34}... | collective-permute-start | bytes 196616 | tf_op jit(solution)/shard_map/ppermute | solution.py:408
  67.0 2.5 %collective-permute-start.1 = (bf16[2,4,32,128]{3,2,1,0:T(8,128)(2,1)S(1)}, bf16[2,4,32,128]{3,2,1,0:T(8,128)(2,1)S(1)}, u32[]{:S(2)}, u32[]{:S(2)}) collective-permute-start(bf16[2,4,32,128]{3,2,1,0:T(8,128)(2,1)S(1)} %get-tuple-element.37), channel_id=1, source_target_pairs={{0,64},{32,96},{64,0},{96,32},{1,65},{33,97},{65,1},{97,33},{2,66}... | collective-permute-start | bytes 196616 | tf_op jit(solution)/shard_map/ppermute | solution.py:408
  69.4 1.1 %collective-permute-start.2 = (bf16[2,4,32,128]{3,2,1,0:T(8,128)(2,1)S(1)}, bf16[2,4,32,128]{3,2,1,0:T(8,128)(2,1)S(1)}, u32[]{:S(2)}, u32[]{:S(2)}) collective-permute-start(bf16[2,4,32,128]{3,2,1,0:T(8,128)(2,1)S(1)} %get-tuple-element.38), channel_id=1, source_target_pairs={{0,96},{32,0},{64,32},{96,64},{1,97},{33,1},{65,33},{97,65},{2,98}... | collective-permute-start | bytes 196616 | tf_op jit(solution)/shard_map/ppermute | solution.py:408
  70.6 0.0 collective-permute-done.refs_5_
  70.6 2.1 %collective-permute-done.1.refs_6_ = bf16[2,4,32,128]{3,2,1,0:T(8,128)(2,1)S(1)} collective-permute-done((bf16[2,4,32,128]{3,2,1,0:T(8,128)(2,1)S(1)}, bf16[2,4,32,128]{3,2,1,0:T(8,128)(2,1)S(1)}, u32[]{:S(2)}, u32[]{:S(2)}) %collective-permute-start.1) | collective-permute-done | bytes 65568 | tf_op jit(solution)/shard_map/ppermute | solution.py:408
  72.7 0.1 collective-permute-done.2.refs_7_
  72.8 1.9 %all-to-all-done.3.refs_0_ = bf16[32,8,512]{2,1,0:T(8,128)(2,1)S(1)} async-done(((bf16[32,8,512]{2,1,0:T(8,128)(2,1)}), bf16[32,8,512]{2,1,0:T(8,128)(2,1)S(1)}, u32[]{:S(2)}, u32[]{:S(2)}) %all-to-all-start.3) | async-done | bytes 262176 | tf_op jit(solution)/shard_map/all_to_all | solution.py:383
  74.8 5.5 %gradients.1 = (bf16[512,4096]{1,0:T(8,128)(2,1)}, f32[4,16,64,128]{3,2,1,0:T(8,128)}) custom-call(bf16[32,8,512]{2,1,0:T(8,128)(2,1)S(1)} %all-to-all-done.3.refs_0_, bf16[256,4096]{1,0:T(8,128)(2,1)S(1)} %copy-done.1, bf16[512,4096]{1,0:T(8,128)(2,1)} %get-tuple-element.34.refs_2_, bf16[64,64]{1,0:T(8,128)(2,1)S(1)} %copy-done.6, ...), custom_call_target="tpu_custom_call" | custom-call | bytes 16777216 | tf_op jit(solution)/shard_map/gradients/pallas_call | solution.py:452
  (6 shorter events, 0.0 us)
Async XLA Ops:
  0.6 22.3 %copy-start = (bf16[4,64,64,128]{3,2,1,0:T(8,128)(2,1)S(1)}, bf16[4,64,64,128]{3,2,1,0:T(8,128)(2,1)}, u32[]{:S(2)}) copy-start(bf16[4,64,64,128]{3,2,1,0:T(8,128)(2,1)} %refs_2_.3) | copy-start | bytes 12582916
  0.6 22.2 %copy-start.3 = (bf16[2,256,128]{2,1,0:T(8,128)(2,1)S(1)}, bf16[2,256,128]{2,1,0:T(8,128)(2,1)}, u32[]{:S(2)}) copy-start(bf16[2,256,128]{2,1,0:T(8,128)(2,1)} %constant.17.clone.refs_4_) | copy-start | bytes 393220
  0.7 22.2 %copy-start.5 = (bf16[2,256,256]{2,1,0:T(8,128)(2,1)S(1)}, bf16[2,256,256]{2,1,0:T(8,128)(2,1)}, u32[]{:S(2)}) copy-start(bf16[2,256,256]{2,1,0:T(8,128)(2,1)} %constant.15.clone.refs_3_) | copy-start | bytes 786436
  0.7 37.1 %copy-start.2 = (bf16[1,8,64,4096]{3,2,1,0:T(8,128)(2,1)S(1)}, bf16[1,8,64,4096]{3,2,1,0:T(8,128)(2,1)}, u32[]{:S(2)}) copy-start(bf16[1,8,64,4096]{3,2,1,0:T(8,128)(2,1)} %param.9) | copy-start | bytes 12582916
  4.2 33.6 %copy-start.1 = (bf16[256,4096]{1,0:T(8,128)(2,1)S(1)}, bf16[256,4096]{1,0:T(8,128)(2,1)}, u32[]{:S(2)}) copy-start(bf16[256,4096]{1,0:T(8,128)(2,1)} %constant.14.clone.table_hbm.table_ref.refs_1_) | copy-start | bytes 6291460
  4.2 33.6 %copy-start.6 = (bf16[64,64]{1,0:T(8,128)(2,1)S(1)}, bf16[64,64]{1,0:T(8,128)(2,1)}, u32[]{:S(2)}) copy-start(bf16[64,64]{1,0:T(8,128)(2,1)} %refs_3_.3) | copy-start | bytes 24580
  37.8 20.3 %copy-start.4 = (bf16[2,256,256]{2,1,0:T(8,128)(2,1)S(1)}, bf16[2,256,256]{2,1,0:T(8,128)(2,1)}, u32[]{:S(2)}) copy-start(bf16[2,256,256]{2,1,0:T(8,128)(2,1)} %constant.16.clone.refs_3_) | copy-start | bytes 786436
  61.8 13.0 %all-to-all-start.3 = ((bf16[32,8,512]{2,1,0:T(8,128)(2,1)}), bf16[32,8,512]{2,1,0:T(8,128)(2,1)S(1)}, u32[]{:S(2)}, u32[]{:S(2)}) async-start(bf16[32,8,512]{2,1,0:T(8,128)(2,1)} %get-tuple-element.33), calls=%async_computation.3 | async-start | bytes 524288 | tf_op jit(solution)/shard_map/all_to_all | solution.py:383
  65.7 4.9 %collective-permute-start = (bf16[2,4,32,128]{3,2,1,0:T(8,128)(2,1)S(1)}, bf16[2,4,32,128]{3,2,1,0:T(8,128)(2,1)S(1)}, u32[]{:S(2)}, u32[]{:S(2)}) collective-permute-start(bf16[2,4,32,128]{3,2,1,0:T(8,128)(2,1)S(1)} %get-tuple-element.36), channel_id=1, source_target_pairs={{0,32},{32,64},{64,96},{96,0},{1,33},{33,65},{65,97},{97,1},{2,34}... | collective-permute-start | bytes 196616 | tf_op jit(solution)/shard_map/ppermute | solution.py:408
  67.0 5.7 %collective-permute-start.1 = (bf16[2,4,32,128]{3,2,1,0:T(8,128)(2,1)S(1)}, bf16[2,4,32,128]{3,2,1,0:T(8,128)(2,1)S(1)}, u32[]{:S(2)}, u32[]{:S(2)}) collective-permute-start(bf16[2,4,32,128]{3,2,1,0:T(8,128)(2,1)S(1)} %get-tuple-element.37), channel_id=1, source_target_pairs={{0,64},{32,96},{64,0},{96,32},{1,65},{33,97},{65,1},{97,33},{2,66}... | collective-permute-start | bytes 196616 | tf_op jit(solution)/shard_map/ppermute | solution.py:408
  69.4 3.4 %collective-permute-start.2 = (bf16[2,4,32,128]{3,2,1,0:T(8,128)(2,1)S(1)}, bf16[2,4,32,128]{3,2,1,0:T(8,128)(2,1)S(1)}, u32[]{:S(2)}, u32[]{:S(2)}) collective-permute-start(bf16[2,4,32,128]{3,2,1,0:T(8,128)(2,1)S(1)} %get-tuple-element.38), channel_id=1, source_target_pairs={{0,96},{32,0},{64,32},{96,64},{1,97},{33,1},{65,33},{97,65},{2,98}... | collective-permute-start | bytes 196616 | tf_op jit(solution)/shard_map/ppermute | solution.py:408

commit v4 on v3

--- a/solution.py
+++ b/solution.py
@@ -132,7 +132,7 @@
             for h in range(width // LANES):
                 block = flat_ref[h, pl.ds(p * mode_rows + i, owners, stride=slots), :]
                 at = (p * (width // LANES) + h) * owners
-                z_ref[i, at : at + owners, :] = block.astype(BF16)
+                z_ref[at : at + owners, i * LANES : (i + 1) * LANES] = block.astype(BF16)
 
 
 def scatter_rows(values, flat_ref, i, owners, slots):
@@ -157,9 +157,11 @@
     gather_rows(got_ref, flat_ref, z_ref)
     count = 2 * kx_count
     stack_rows = 2 * STACK
+    first = dot_nn(rows_ref[0], z_ref[...])
+    second = dot_nn(rows_ref[1], z_ref[...])
     for i in range(mode_rows):
-        z = z_ref[i]
-        both = fold(dot_nn(rows_ref[0], z), dot_nn(rows_ref[1], z))
+        lanes = slice(i * LANES, (i + 1) * LANES)
+        both = fold(first[:, lanes], second[:, lanes])
         if adjoint:
             plain, turned = both[:count], both[count:]
             left = jnp.where(half_mask(plain.shape), plain, turned)
@@ -173,7 +175,7 @@
                 full = dot_nt(pair, w)[g % 2 * stack_rows : (g % 2 + 1) * stack_rows]
                 picked = jnp.where(row < 2, full[:, :LANES], full[:, LANES:])
                 picked = jnp.where((row % 2 == 0) == low, picked, 0.0)
-                y_ref[g * stack_rows : (g + 1) * stack_rows, :] = picked + pltpu.roll(
+                y_ref[g * stack_rows : (g + 1) * stack_rows, lanes] = picked + pltpu.roll(
                     picked, LANES // 2, 1
                 )
         else:
@@ -186,13 +188,14 @@
                 mode_ref[i, g * stack_rows : (g + 1) * stack_rows, :] = both[rows][:stack_rows]
                 w = weight_ref[i, g * STACK : (g + 1) * STACK].reshape(STACK * channels, LANES)
                 full = dot_nn(left[rows], w)
-                y_ref[g * stack_rows : (g + 1) * stack_rows, :] = fold(
+                y_ref[g * stack_rows : (g + 1) * stack_rows, lanes] = fold(
                     full[:stack_rows], full[stack_rows:]
                 )
-        y = y_ref[...].astype(BF16)
-        low = half_mask((back_ref.shape[1], LANES))
-        values = jnp.where(low, dot_nn(back_ref[0], y), dot_nn(back_ref[1], y))
-        scatter_rows(values, flat_ref, i, owners, slots)
+    y = y_ref[...].astype(BF16)
+    first, second = dot_nn(back_ref[0], y), dot_nn(back_ref[1], y)
+    values = jnp.where(half_mask(first.shape), first, second)
+    for i in range(mode_rows):
+        scatter_rows(values[:, i * LANES : (i + 1) * LANES], flat_ref, i, owners, slots)
     for h in range(flat_ref.shape[0]):
         part = flat_ref[h].reshape(owners, slots, LANES)
         sent_ref[:, :, h * LANES : (h + 1) * LANES] = part.astype(BF16)
@@ -393,9 +396,9 @@
             out_specs=[VMEM] * (1 + samples),
             scratch_shapes=[
                 pltpu.VMEM((lines // LANES, groups * slots, LANES), F32),
-                pltpu.VMEM((mode_rows, rows_here * groups, LANES), BF16),
+                pltpu.VMEM((rows_here * groups, mode_rows * LANES), BF16),
                 pltpu.VMEM((mode_rows, 2 * kx_count, LANES), F32),
-                pltpu.VMEM((2 * kx_count, LANES), F32),
+                pltpu.VMEM((2 * kx_count, mode_rows * LANES), F32),
             ],
             compiler_params=params(10),
             cost_estimate=cost(16),

time: 80.8 us -> 78.5 us (0.972)
  Pallas kernels: 23 us -> 20.9 us
    pallas_call x2, Pallas kernels: 6.15 us -> 4.06 us  [mix(): pl.pallas_call(lambda *refs: modes_kernel(*refs, adjoint=adjoint, samples...]
where the time goes in v4:
time: 78.5 us; the launch traced here: 78.2 us
  blocking collectives  43.6 us (56%)
  Pallas kernels  20.9 us (27%)
  starting transfers between devices  8.77 us (11%)
  waiting for transfers between devices  4.04 us (5%)
  between operations  0.9 us (1%)
    all_to_all x3, blocking collectives, exchange(): return lax.all_to_all(values, 'space', 0, 0, tiled=True)  43.6 us
    pallas_call x1, Pallas kernels, on_device(): pl.pallas_call(field_kernel, out_shape=[lines_shape, lines_shape, exchang...  7.8 us
    pallas_call x1, Pallas kernels, on_device(): pl.pallas_call(lambda *refs: grad_kernel(*refs, samples=samples), out_sha...  5.53 us
    ppermute x3, starting transfers between devices, share(): lax.ppermute(blocks[k], 'dp', [(a, (a + k) % samples) for a in range(samp...  5.06 us
    pallas_call x2, Pallas kernels, mix(): pl.pallas_call(lambda *refs: modes_kernel(*refs, adjoint=adjoint, samples...  4.06 us
    all_to_all x1, starting transfers between devices, exchange(): return lax.all_to_all(values, 'space', 0, 0, tiled=True)  3.71 us
    pallas_call x1, Pallas kernels, on_device(): pl.pallas_call(columns_kernel, out_shape=[exchange_shape, jax.ShapeDtypeS...  3.52 us
    ppermute x3, waiting for transfers between devices, share(): lax.ppermute(blocks[k], 'dp', [(a, (a + k) % samples) for a in range(samp...  2.26 us
  transfers between devices with their start and end apart: 4, of which 3 were waited for; matrix products, arithmetic and copies ran while one was open for 0% of the time, Pallas kernels for 0%

profile of v4, /device:TPU:1, one launch (start us, length us, event | category | flops | bytes accessed | tf_op | source)
XLA Modules:
  0.0 78.2 jit_solution(15387296023714701255)
XLA Ops:
  0.6 0.0 copy-start.3
  0.7 0.0 copy-start.5
  0.7 0.0 copy-start.2
  0.7 3.5 %columns.1 = (bf16[32,8,512]{2,1,0:T(8,128)(2,1)S(1)}, bf16[512,4096]{1,0:T(8,128)(2,1)S(1)}) custom-call(bf16[256,4096]{1,0:T(8,128)(2,1)} %constant.14.clone.table_hbm.table_ref.refs_1_, bf16[512,4096]{1,0:T(8,128)(2,1)} %bitcast.7, bf16[512,4096]{1,0:T(8,128)(2,1)} %bitcast.5, bf16[4,64,64,128]{3,2,1,0:T(8,128)(2,1)} %refs_2_.3), custom_call_target="tpu_custom_call" | custom-call | bytes 16777216 | tf_op jit(solution)/shard_map/columns/pallas_call | solution.py:417
  4.2 0.0 copy-start.1
  4.2 0.0 copy-start.6
  4.2 18.7 %all_to_all.20.refs_1_ = bf16[32,8,512]{2,1,0:T(8,128)(2,1)S(1)} all-to-all(bf16[32,8,512]{2,1,0:T(8,128)(2,1)S(1)} %get-tuple-element.24), channel_id=1, replica_groups=mesh['dp'=4,'space'=32] {'space'}, dimensions={0} | all-to-all | bytes 524288 | tf_op jit(solution)/shard_map/all_to_all | solution.py:386
  22.9 0.0 copy-done.5
  22.9 1.4 %mix_modes.1 = (bf16[32,8,512]{2,1,0:T(8,128)(2,1)S(1)}, bf16[4,32,128]{2,1,0:T(8,128)(2,1)S(1)}, bf16[4,32,128]{2,1,0:T(8,128)(2,1)S(1)}, bf16[4,32,128]{2,1,0:T(8,128)(2,1)S(1)}, bf16[4,32,128]{2,1,0:T(8,128)(2,1)S(1)}) custom-call(s32[1]{0:T(128)} %bitcast.2.refs_0_, bf16[32,8,512]{2,1,0:T(8,128)(2,1)S(1)} %all_to_all.20.refs_1_, ...), custom_call_target="tpu_custom_call" | custom-call | bytes 16777216 | tf_op jit(solution)/shard_map/mix_modes/pallas_call | solution.py:392
  24.3 12.5 %all_to_all.21.back_ref = bf16[32,8,512]{2,1,0:T(8,128)(2,1)S(1)} all-to-all(bf16[32,8,512]{2,1,0:T(8,128)(2,1)S(1)} %get-tuple-element.25), channel_id=1, replica_groups=mesh['dp'=4,'space'=32] {'space'}, dimensions={0} | all-to-all | bytes 524288 | tf_op jit(solution)/shard_map/all_to_all | solution.py:386
  36.8 0.0 copy-start.4
  36.8 7.8 %field_step.1 = (bf16[512,4096]{1,0:T(8,128)(2,1)}, bf16[512,4096]{1,0:T(8,128)(2,1)}, bf16[32,8,512]{2,1,0:T(8,128)(2,1)S(1)}) custom-call(bf16[32,8,512]{2,1,0:T(8,128)(2,1)S(1)} %all_to_all.21.back_ref, bf16[256,4096]{1,0:T(8,128)(2,1)S(1)} %copy-done.1, bf16[512,4096]{1,0:T(8,128)(2,1)S(1)} %get-tuple-element.26.fields_ref, ...), custom_call_target="tpu_custom_call" | custom-call | bytes 25165824 | tf_op jit(solution)/shard_map/field_step/pallas_call | solution.py:434
  44.6 12.5 %all_to_all.22.refs_1_ = bf16[32,8,512]{2,1,0:T(8,128)(2,1)S(1)} all-to-all(bf16[32,8,512]{2,1,0:T(8,128)(2,1)S(1)} %get-tuple-element.28), channel_id=1, replica_groups=mesh['dp'=4,'space'=32] {'space'}, dimensions={0} | all-to-all | bytes 524288 | tf_op jit(solution)/shard_map/all_to_all | solution.py:386
  57.1 0.0 copy-done.4
  57.1 2.7 %adjoint_modes.1 = (bf16[32,8,512]{2,1,0:T(8,128)(2,1)}, bf16[2,4,32,128]{3,2,1,0:T(8,128)(2,1)S(1)}, bf16[2,4,32,128]{3,2,1,0:T(8,128)(2,1)S(1)}, bf16[2,4,32,1...) custom-call(s32[1]{0:T(128)} %bitcast.2.refs_0_, bf16[32,8,512]{2,1,0:T(8,128)(2,1)S(1)} %all_to_all.22.refs_1_, ...), custom_call_target="tpu_custom_call" | custom-call | bytes 16777216 | tf_op jit(solution)/shard_map/adjoint_modes/pallas_call | solution.py:392
  59.7 3.7 %all-to-all-start.3 = ((bf16[32,8,512]{2,1,0:T(8,128)(2,1)}), bf16[32,8,512]{2,1,0:T(8,128)(2,1)S(1)}, u32[]{:S(2)}, u32[]{:S(2)}) async-start(bf16[32,8,512]{2,1,0:T(8,128)(2,1)} %get-tuple-element.33), calls=%async_computation.3 | async-start | bytes 524288 | tf_op jit(solution)/shard_map/all_to_all | solution.py:386
  63.4 1.5 %collective-permute-start = (bf16[2,4,32,128]{3,2,1,0:T(8,128)(2,1)S(1)}, bf16[2,4,32,128]{3,2,1,0:T(8,128)(2,1)S(1)}, u32[]{:S(2)}, u32[]{:S(2)}) collective-permute-start(bf16[2,4,32,128]{3,2,1,0:T(8,128)(2,1)S(1)} %get-tuple-element.36), channel_id=1, source_target_pairs={{0,32},{32,64},{64,96},{96,0},{1,33},{33,65},{65,97},{97,1},{2,34}... | collective-permute-start | bytes 196616 | tf_op jit(solution)/shard_map/ppermute | solution.py:411
  64.9 2.5 %collective-permute-start.1 = (bf16[2,4,32,128]{3,2,1,0:T(8,128)(2,1)S(1)}, bf16[2,4,32,128]{3,2,1,0:T(8,128)(2,1)S(1)}, u32[]{:S(2)}, u32[]{:S(2)}) collective-permute-start(bf16[2,4,32,128]{3,2,1,0:T(8,128)(2,1)S(1)} %get-tuple-element.37), channel_id=1, source_target_pairs={{0,64},{32,96},{64,0},{96,32},{1,65},{33,97},{65,1},{97,33},{2,66}... | collective-permute-start | bytes 196616 | tf_op jit(solution)/shard_map/ppermute | solution.py:411
  67.3 1.1 %collective-permute-start.2 = (bf16[2,4,32,128]{3,2,1,0:T(8,128)(2,1)S(1)}, bf16[2,4,32,128]{3,2,1,0:T(8,128)(2,1)S(1)}, u32[]{:S(2)}, u32[]{:S(2)}) collective-permute-start(bf16[2,4,32,128]{3,2,1,0:T(8,128)(2,1)S(1)} %get-tuple-element.38), channel_id=1, source_target_pairs={{0,96},{32,0},{64,32},{96,64},{1,97},{33,1},{65,33},{97,65},{2,98}... | collective-permute-start | bytes 196616 | tf_op jit(solution)/shard_map/ppermute | solution.py:411
  68.5 0.0 collective-permute-done.refs_5_
  68.5 2.1 %collective-permute-done.1.refs_6_ = bf16[2,4,32,128]{3,2,1,0:T(8,128)(2,1)S(1)} collective-permute-done((bf16[2,4,32,128]{3,2,1,0:T(8,128)(2,1)S(1)}, bf16[2,4,32,128]{3,2,1,0:T(8,128)(2,1)S(1)}, u32[]{:S(2)}, u32[]{:S(2)}) %collective-permute-start.1) | collective-permute-done | bytes 65568 | tf_op jit(solution)/shard_map/ppermute | solution.py:411
  70.6 0.1 collective-permute-done.2.refs_7_
  70.8 1.8 %all-to-all-done.3.refs_0_ = bf16[32,8,512]{2,1,0:T(8,128)(2,1)S(1)} async-done(((bf16[32,8,512]{2,1,0:T(8,128)(2,1)}), bf16[32,8,512]{2,1,0:T(8,128)(2,1)S(1)}, u32[]{:S(2)}, u32[]{:S(2)}) %all-to-all-start.3) | async-done | bytes 262176 | tf_op jit(solution)/shard_map/all_to_all | solution.py:386
  72.5 5.5 %gradients.1 = (bf16[512,4096]{1,0:T(8,128)(2,1)}, f32[4,16,64,128]{3,2,1,0:T(8,128)}) custom-call(bf16[32,8,512]{2,1,0:T(8,128)(2,1)S(1)} %all-to-all-done.3.refs_0_, bf16[256,4096]{1,0:T(8,128)(2,1)S(1)} %copy-done.1, bf16[512,4096]{1,0:T(8,128)(2,1)} %get-tuple-element.34.refs_2_, bf16[64,64]{1,0:T(8,128)(2,1)S(1)} %copy-done.6, ...), custom_call_target="tpu_custom_call" | custom-call | bytes 16777216 | tf_op jit(solution)/shard_map/gradients/pallas_call | solution.py:455
  (6 shorter events, 0.0 us)
Async XLA Ops:
  0.6 22.3 %copy-start = (bf16[4,64,64,128]{3,2,1,0:T(8,128)(2,1)S(1)}, bf16[4,64,64,128]{3,2,1,0:T(8,128)(2,1)}, u32[]{:S(2)}) copy-start(bf16[4,64,64,128]{3,2,1,0:T(8,128)(2,1)} %refs_2_.3) | copy-start | bytes 12582916
  0.6 22.2 %copy-start.3 = (bf16[2,256,128]{2,1,0:T(8,128)(2,1)S(1)}, bf16[2,256,128]{2,1,0:T(8,128)(2,1)}, u32[]{:S(2)}) copy-start(bf16[2,256,128]{2,1,0:T(8,128)(2,1)} %constant.17.clone.refs_4_) | copy-start | bytes 393220
  0.7 22.2 %copy-start.5 = (bf16[2,256,256]{2,1,0:T(8,128)(2,1)S(1)}, bf16[2,256,256]{2,1,0:T(8,128)(2,1)}, u32[]{:S(2)}) copy-start(bf16[2,256,256]{2,1,0:T(8,128)(2,1)} %constant.15.clone.refs_3_) | copy-start | bytes 786436
  0.7 36.1 %copy-start.2 = (bf16[1,8,64,4096]{3,2,1,0:T(8,128)(2,1)S(1)}, bf16[1,8,64,4096]{3,2,1,0:T(8,128)(2,1)}, u32[]{:S(2)}) copy-start(bf16[1,8,64,4096]{3,2,1,0:T(8,128)(2,1)} %param.9) | copy-start | bytes 12582916
  4.2 32.6 %copy-start.1 = (bf16[256,4096]{1,0:T(8,128)(2,1)S(1)}, bf16[256,4096]{1,0:T(8,128)(2,1)}, u32[]{:S(2)}) copy-start(bf16[256,4096]{1,0:T(8,128)(2,1)} %constant.14.clone.table_hbm.table_ref.refs_1_) | copy-start | bytes 6291460
  4.2 32.6 %copy-start.6 = (bf16[64,64]{1,0:T(8,128)(2,1)S(1)}, bf16[64,64]{1,0:T(8,128)(2,1)}, u32[]{:S(2)}) copy-start(bf16[64,64]{1,0:T(8,128)(2,1)} %refs_3_.3) | copy-start | bytes 24580
  36.8 20.3 %copy-start.4 = (bf16[2,256,256]{2,1,0:T(8,128)(2,1)S(1)}, bf16[2,256,256]{2,1,0:T(8,128)(2,1)}, u32[]{:S(2)}) copy-start(bf16[2,256,256]{2,1,0:T(8,128)(2,1)} %constant.16.clone.refs_3_) | copy-start | bytes 786436
  59.7 12.8 %all-to-all-start.3 = ((bf16[32,8,512]{2,1,0:T(8,128)(2,1)}), bf16[32,8,512]{2,1,0:T(8,128)(2,1)S(1)}, u32[]{:S(2)}, u32[]{:S(2)}) async-start(bf16[32,8,512]{2,1,0:T(8,128)(2,1)} %get-tuple-element.33), calls=%async_computation.3 | async-start | bytes 524288 | tf_op jit(solution)/shard_map/all_to_all | solution.py:386
  63.4 5.1 %collective-permute-start = (bf16[2,4,32,128]{3,2,1,0:T(8,128)(2,1)S(1)}, bf16[2,4,32,128]{3,2,1,0:T(8,128)(2,1)S(1)}, u32[]{:S(2)}, u32[]{:S(2)}) collective-permute-start(bf16[2,4,32,128]{3,2,1,0:T(8,128)(2,1)S(1)} %get-tuple-element.36), channel_id=1, source_target_pairs={{0,32},{32,64},{64,96},{96,0},{1,33},{33,65},{65,97},{97,1},{2,34}... | collective-permute-start | bytes 196616 | tf_op jit(solution)/shard_map/ppermute | solution.py:411
  64.9 5.7 %collective-permute-start.1 = (bf16[2,4,32,128]{3,2,1,0:T(8,128)(2,1)S(1)}, bf16[2,4,32,128]{3,2,1,0:T(8,128)(2,1)S(1)}, u32[]{:S(2)}, u32[]{:S(2)}) collective-permute-start(bf16[2,4,32,128]{3,2,1,0:T(8,128)(2,1)S(1)} %get-tuple-element.37), channel_id=1, source_target_pairs={{0,64},{32,96},{64,0},{96,32},{1,65},{33,97},{65,1},{97,33},{2,66}... | collective-permute-start | bytes 196616 | tf_op jit(solution)/shard_map/ppermute | solution.py:411
  67.3 3.4 %collective-permute-start.2 = (bf16[2,4,32,128]{3,2,1,0:T(8,128)(2,1)S(1)}, bf16[2,4,32,128]{3,2,1,0:T(8,128)(2,1)S(1)}, u32[]{:S(2)}, u32[]{:S(2)}) collective-permute-start(bf16[2,4,32,128]{3,2,1,0:T(8,128)(2,1)S(1)} %get-tuple-element.38), channel_id=1, source_target_pairs={{0,96},{32,0},{64,32},{96,64},{1,97},{33,1},{65,33},{97,65},{2,98}... | collective-permute-start | bytes 196616 | tf_op jit(solution)/shard_map/ppermute | solution.py:411

commit v5 on v4

--- a/solution.py
+++ b/solution.py
@@ -212,12 +212,13 @@
                 shared_ref[i] = values
 
 
-def transposed_back(back_ref, mode_rows, weighted):
+def transpose_back(back_ref, turned_ref, mode_rows, weighted):
     owners, slots, width = back_ref.shape
-    flat = back_ref[...].astype(F32).reshape(owners * slots, width)
-    if weighted:
-        flat = weigh(flat, mode_rows)
-    return flat.T.astype(BF16)
+    for at in range(0, width, DIAGONAL):
+        flat = back_ref[:, :, at : at + DIAGONAL].astype(F32).reshape(owners * slots, DIAGONAL)
+        if weighted:
+            flat = weigh(flat, mode_rows)
+        turned_ref[at : at + DIAGONAL, :] = flat.T.astype(BF16)
 
 
 def spread(block, out_ref):
@@ -230,12 +231,14 @@
 def gelu_chunk(pre_ref, upstream_ref, response_ref, delta_ref, slot, rows, cols):
     v = pre_ref[slot, rows, :]
     t = jnp.tanh(v * (GELU_SCALE + (GELU_SCALE * GELU_CUBIC) * (v * v)))
-    half = (0.5 + 0.5 * t).astype(BF16)
-    rest = (1.0 - t * t).astype(BF16)
+    scaled = 0.5 * t
+    half = (0.5 + scaled).astype(BF16)
+    other = (0.5 - scaled).astype(BF16)
     v = v.astype(BF16)
-    response_ref[rows, cols] = v * half
-    inner = (0.5 * GELU_SCALE) + (1.5 * GELU_SCALE * GELU_CUBIC) * (v * v)
-    delta_ref[rows, cols] = upstream_ref[rows, cols] * (half + v * rest * inner)
+    value = v * half
+    response_ref[rows, cols] = value
+    inner = (2.0 * GELU_SCALE) + (6.0 * GELU_SCALE * GELU_CUBIC) * (v * v)
+    delta_ref[rows, cols] = upstream_ref[rows, cols] * (half + value * other * inner)
 
 
 def field_kernel(
@@ -244,8 +247,8 @@
     response_ref, delta_ref, turned_ref, mix_ref, pre_ref, acc_ref, sem_ref,
 ):
     mode_rows = back_ref.shape[1] // 2
-    turned_ref[...] = transposed_back(back_ref, mode_rows, True)
     spread(weight_ref[...].astype(F32).T.astype(BF16), mix_ref)
+    transpose_back(back_ref, turned_ref, mode_rows, True)
     width = mix_ref.shape[0]
     total = fields_ref.shape[0]
     chunk = 32
@@ -306,26 +309,28 @@
     shared_refs, (out_hbm, modes_hbm) = rest[:samples], rest[samples : samples + 2]
     delta_ref, turned_ref, mix_ref, out_ref, modes_ref, sem_ref = rest[samples + 2 :]
     loads = Loads(((delta_hbm, delta_ref),), sem_ref, LOAD_TILE)
-    turned_ref[...] = transposed_back(back_ref, 0, False)
     spread(weight_ref[...], mix_ref)
+    transpose_back(back_ref, turned_ref, 0, False)
     width = mix_ref.shape[0]
     copies = []
     for i in range(modes_ref.shape[0]):
         mode_products(shared_refs, modes_ref, i)
-        copies.append(pltpu.make_async_copy(modes_ref.at[i], modes_hbm.at[i], sem_ref.at[2, i]))
+        copies.append(pltpu.make_async_copy(modes_ref.at[i], modes_hbm.at[i], sem_ref.at[1, i]))
         copies[-1].start()
     for k, cols in enumerate(tiles(table_ref.shape[1], LOAD_TILE)):
         loads.wait(k)
-        for at in range(0, delta_ref.shape[0], width):
+        for n, at in enumerate(range(0, delta_ref.shape[0], width)):
             rows = slice(at, at + width)
             out_ref[rows, cols] = (
                 dot_nn(turned_ref[rows, :], table_ref[:, cols])
                 + dot_nn(mix_ref[...], delta_ref[rows, cols])
             ).astype(BF16)
-        copies.append(
-            pltpu.make_async_copy(out_ref.at[:, cols], out_hbm.at[:, cols], sem_ref.at[1, k])
-        )
-        copies[-1].start()
+            copies.append(
+                pltpu.make_async_copy(
+                    out_ref.at[rows, cols], out_hbm.at[rows, cols], sem_ref.at[2 + n, k]
+                )
+            )
+            copies[-1].start()
     for copy in copies:
         copy.wait()
 
@@ -463,7 +468,9 @@
             pltpu.VMEM((DIAGONAL, DIAGONAL), BF16),
             pltpu.VMEM((lines, length), BF16),
             pltpu.VMEM(modes_shape.shape, F32),
-            pltpu.SemaphoreType.DMA((3, max(length // LOAD_TILE, mode_rows))),
+            pltpu.SemaphoreType.DMA(
+                (2 + lines // DIAGONAL, max(length // LOAD_TILE, mode_rows))
+            ),
         ],
         compiler_params=params(20),
         cost_estimate=cost(16),

time: 78.5 us -> 78 us (level)
  no operation moved by 1% of the time
where the time goes in v5:
time: 78 us; the launch traced here: 77.7 us
  blocking collectives  43.6 us (56%)
  Pallas kernels  20.4 us (26%)
  starting transfers between devices  8.77 us (11%)
  waiting for transfers between devices  4.04 us (5%)
  between operations  0.9 us (1%)
    all_to_all x3, blocking collectives, exchange(): return lax.all_to_all(values, 'space', 0, 0, tiled=True)  43.6 us
    pallas_call x1, Pallas kernels, on_device(): pl.pallas_call(field_kernel, out_shape=[lines_shape, lines_shape, exchang...  7.45 us
    pallas_call x1, Pallas kernels, on_device(): pl.pallas_call(lambda *refs: grad_kernel(*refs, samples=samples), out_sha...  5.39 us
    ppermute x3, starting transfers between devices, share(): lax.ppermute(blocks[k], 'dp', [(a, (a + k) % samples) for a in range(samp...  5.06 us
    pallas_call x2, Pallas kernels, mix(): pl.pallas_call(lambda *refs: modes_kernel(*refs, adjoint=adjoint, samples...  4.06 us
    all_to_all x1, starting transfers between devices, exchange(): return lax.all_to_all(values, 'space', 0, 0, tiled=True)  3.71 us
    pallas_call x1, Pallas kernels, on_device(): pl.pallas_call(columns_kernel, out_shape=[exchange_shape, jax.ShapeDtypeS...  3.52 us
    ppermute x3, waiting for transfers between devices, share(): lax.ppermute(blocks[k], 'dp', [(a, (a + k) % samples) for a in range(samp...  2.27 us
  transfers between devices with their start and end apart: 4, of which 3 were waited for; matrix products, arithmetic and copies ran while one was open for 0% of the time, Pallas kernels for 0%

profile of v5, /device:TPU:1, one launch (start us, length us, event | category | flops | bytes accessed | tf_op | source)
XLA Modules:
  0.0 77.7 jit_solution(7582940541415880890)
XLA Ops:
  0.6 0.0 copy-start.3
  0.7 0.0 copy-start.5
  0.7 3.5 %columns.1 = (bf16[32,8,512]{2,1,0:T(8,128)(2,1)S(1)}, bf16[512,4096]{1,0:T(8,128)(2,1)S(1)}) custom-call(bf16[256,4096]{1,0:T(8,128)(2,1)} %constant.14.clone.table_hbm.table_ref.refs_1_, bf16[512,4096]{1,0:T(8,128)(2,1)} %bitcast.7, bf16[512,4096]{1,0:T(8,128)(2,1)} %bitcast.5, bf16[4,64,64,128]{3,2,1,0:T(8,128)(2,1)} %refs_2_.3), custom_call_target="tpu_custom_call" | custom-call | bytes 16777216 | tf_op jit(solution)/shard_map/columns/pallas_call | solution.py:422
  4.2 0.0 copy-start.1
  4.2 0.0 copy-start.6
  4.2 18.7 %all_to_all.20.refs_1_ = bf16[32,8,512]{2,1,0:T(8,128)(2,1)S(1)} all-to-all(bf16[32,8,512]{2,1,0:T(8,128)(2,1)S(1)} %get-tuple-element.24), channel_id=1, replica_groups=mesh['dp'=4,'space'=32] {'space'}, dimensions={0} | all-to-all | bytes 524288 | tf_op jit(solution)/shard_map/all_to_all | solution.py:391
  22.9 0.0 copy-done.3
  22.9 1.4 %mix_modes.1 = (bf16[32,8,512]{2,1,0:T(8,128)(2,1)S(1)}, bf16[4,32,128]{2,1,0:T(8,128)(2,1)S(1)}, bf16[4,32,128]{2,1,0:T(8,128)(2,1)S(1)}, bf16[4,32,128]{2,1,0:T(8,128)(2,1)S(1)}, bf16[4,32,128]{2,1,0:T(8,128)(2,1)S(1)}) custom-call(s32[1]{0:T(128)} %bitcast.2.refs_0_, bf16[32,8,512]{2,1,0:T(8,128)(2,1)S(1)} %all_to_all.20.refs_1_, ...), custom_call_target="tpu_custom_call" | custom-call | bytes 16777216 | tf_op jit(solution)/shard_map/mix_modes/pallas_call | solution.py:397
  24.3 12.5 %all_to_all.21.back_ref = bf16[32,8,512]{2,1,0:T(8,128)(2,1)S(1)} all-to-all(bf16[32,8,512]{2,1,0:T(8,128)(2,1)S(1)} %get-tuple-element.25), channel_id=1, replica_groups=mesh['dp'=4,'space'=32] {'space'}, dimensions={0} | all-to-all | bytes 524288 | tf_op jit(solution)/shard_map/all_to_all | solution.py:391
  36.8 0.0 copy-done.2
  36.8 0.0 copy-done.6
  36.8 0.0 copy-start.4
  36.8 7.5 %field_step.1 = (bf16[512,4096]{1,0:T(8,128)(2,1)}, bf16[512,4096]{1,0:T(8,128)(2,1)}, bf16[32,8,512]{2,1,0:T(8,128)(2,1)S(1)}) custom-call(bf16[32,8,512]{2,1,0:T(8,128)(2,1)S(1)} %all_to_all.21.back_ref, bf16[256,4096]{1,0:T(8,128)(2,1)S(1)} %copy-done.1, bf16[512,4096]{1,0:T(8,128)(2,1)S(1)} %get-tuple-element.26.fields_ref, ...), custom_call_target="tpu_custom_call" | custom-call | bytes 25165824 | tf_op jit(solution)/shard_map/field_step/pallas_call | solution.py:439
  44.2 12.4 %all_to_all.22.refs_1_ = bf16[32,8,512]{2,1,0:T(8,128)(2,1)S(1)} all-to-all(bf16[32,8,512]{2,1,0:T(8,128)(2,1)S(1)} %get-tuple-element.28), channel_id=1, replica_groups=mesh['dp'=4,'space'=32] {'space'}, dimensions={0} | all-to-all | bytes 524288 | tf_op jit(solution)/shard_map/all_to_all | solution.py:391
  56.7 2.7 %adjoint_modes.1 = (bf16[32,8,512]{2,1,0:T(8,128)(2,1)}, bf16[2,4,32,128]{3,2,1,0:T(8,128)(2,1)S(1)}, bf16[2,4,32,128]{3,2,1,0:T(8,128)(2,1)S(1)}, bf16[2,4,32,1...) custom-call(s32[1]{0:T(128)} %bitcast.2.refs_0_, bf16[32,8,512]{2,1,0:T(8,128)(2,1)S(1)} %all_to_all.22.refs_1_, ...), custom_call_target="tpu_custom_call" | custom-call | bytes 16777216 | tf_op jit(solution)/shard_map/adjoint_modes/pallas_call | solution.py:397
  59.4 3.7 %all-to-all-start.3 = ((bf16[32,8,512]{2,1,0:T(8,128)(2,1)}), bf16[32,8,512]{2,1,0:T(8,128)(2,1)S(1)}, u32[]{:S(2)}, u32[]{:S(2)}) async-start(bf16[32,8,512]{2,1,0:T(8,128)(2,1)} %get-tuple-element.33), calls=%async_computation.3 | async-start | bytes 524288 | tf_op jit(solution)/shard_map/all_to_all | solution.py:391
  63.1 1.5 %collective-permute-start = (bf16[2,4,32,128]{3,2,1,0:T(8,128)(2,1)S(1)}, bf16[2,4,32,128]{3,2,1,0:T(8,128)(2,1)S(1)}, u32[]{:S(2)}, u32[]{:S(2)}) collective-permute-start(bf16[2,4,32,128]{3,2,1,0:T(8,128)(2,1)S(1)} %get-tuple-element.36), channel_id=1, source_target_pairs={{0,32},{32,64},{64,96},{96,0},{1,33},{33,65},{65,97},{97,1},{2,34}... | collective-permute-start | bytes 196616 | tf_op jit(solution)/shard_map/ppermute | solution.py:416
  64.5 2.5 %collective-permute-start.1 = (bf16[2,4,32,128]{3,2,1,0:T(8,128)(2,1)S(1)}, bf16[2,4,32,128]{3,2,1,0:T(8,128)(2,1)S(1)}, u32[]{:S(2)}, u32[]{:S(2)}) collective-permute-start(bf16[2,4,32,128]{3,2,1,0:T(8,128)(2,1)S(1)} %get-tuple-element.37), channel_id=1, source_target_pairs={{0,64},{32,96},{64,0},{96,32},{1,65},{33,97},{65,1},{97,33},{2,66}... | collective-permute-start | bytes 196616 | tf_op jit(solution)/shard_map/ppermute | solution.py:416
  67.0 1.1 %collective-permute-start.2 = (bf16[2,4,32,128]{3,2,1,0:T(8,128)(2,1)S(1)}, bf16[2,4,32,128]{3,2,1,0:T(8,128)(2,1)S(1)}, u32[]{:S(2)}, u32[]{:S(2)}) collective-permute-start(bf16[2,4,32,128]{3,2,1,0:T(8,128)(2,1)S(1)} %get-tuple-element.38), channel_id=1, source_target_pairs={{0,96},{32,0},{64,32},{96,64},{1,97},{33,1},{65,33},{97,65},{2,98}... | collective-permute-start | bytes 196616 | tf_op jit(solution)/shard_map/ppermute | solution.py:416
  68.1 0.0 collective-permute-done.refs_5_
  68.1 2.1 %collective-permute-done.1.refs_6_ = bf16[2,4,32,128]{3,2,1,0:T(8,128)(2,1)S(1)} collective-permute-done((bf16[2,4,32,128]{3,2,1,0:T(8,128)(2,1)S(1)}, bf16[2,4,32,128]{3,2,1,0:T(8,128)(2,1)S(1)}, u32[]{:S(2)}, u32[]{:S(2)}) %collective-permute-start.1) | collective-permute-done | bytes 65568 | tf_op jit(solution)/shard_map/ppermute | solution.py:416
  70.3 0.1 collective-permute-done.2.refs_7_
  70.4 1.8 %all-to-all-done.3.refs_0_ = bf16[32,8,512]{2,1,0:T(8,128)(2,1)S(1)} async-done(((bf16[32,8,512]{2,1,0:T(8,128)(2,1)}), bf16[32,8,512]{2,1,0:T(8,128)(2,1)S(1)}, u32[]{:S(2)}, u32[]{:S(2)}) %all-to-all-start.3) | async-done | bytes 262176 | tf_op jit(solution)/shard_map/all_to_all | solution.py:391
  72.2 5.4 %gradients.1 = (bf16[512,4096]{1,0:T(8,128)(2,1)}, f32[4,16,64,128]{3,2,1,0:T(8,128)}) custom-call(bf16[32,8,512]{2,1,0:T(8,128)(2,1)S(1)} %all-to-all-done.3.refs_0_, bf16[256,4096]{1,0:T(8,128)(2,1)S(1)} %copy-done.1, bf16[512,4096]{1,0:T(8,128)(2,1)} %get-tuple-element.34.refs_2_, bf16[64,64]{1,0:T(8,128)(2,1)S(1)} %copy-done.6, ...), custom_call_target="tpu_custom_call" | custom-call | bytes 16777216 | tf_op jit(solution)/shard_map/gradients/pallas_call | solution.py:460
  (6 shorter events, 0.0 us)
Async XLA Ops:
  0.6 22.3 %copy-start = (bf16[4,64,64,128]{3,2,1,0:T(8,128)(2,1)S(1)}, bf16[4,64,64,128]{3,2,1,0:T(8,128)(2,1)}, u32[]{:S(2)}) copy-start(bf16[4,64,64,128]{3,2,1,0:T(8,128)(2,1)} %refs_2_.3) | copy-start | bytes 12582916
  0.6 22.2 %copy-start.3 = (bf16[2,256,128]{2,1,0:T(8,128)(2,1)S(1)}, bf16[2,256,128]{2,1,0:T(8,128)(2,1)}, u32[]{:S(2)}) copy-start(bf16[2,256,128]{2,1,0:T(8,128)(2,1)} %constant.17.clone.refs_4_) | copy-start | bytes 393220
  0.7 22.2 %copy-start.5 = (bf16[2,256,256]{2,1,0:T(8,128)(2,1)S(1)}, bf16[2,256,256]{2,1,0:T(8,128)(2,1)}, u32[]{:S(2)}) copy-start(bf16[2,256,256]{2,1,0:T(8,128)(2,1)} %constant.15.clone.refs_3_) | copy-start | bytes 786436
  0.7 36.1 %copy-start.2 = (bf16[1,8,64,4096]{3,2,1,0:T(8,128)(2,1)S(1)}, bf16[1,8,64,4096]{3,2,1,0:T(8,128)(2,1)}, u32[]{:S(2)}) copy-start(bf16[1,8,64,4096]{3,2,1,0:T(8,128)(2,1)} %param.9) | copy-start | bytes 12582916
  4.2 32.6 %copy-start.1 = (bf16[256,4096]{1,0:T(8,128)(2,1)S(1)}, bf16[256,4096]{1,0:T(8,128)(2,1)}, u32[]{:S(2)}) copy-start(bf16[256,4096]{1,0:T(8,128)(2,1)} %constant.14.clone.table_hbm.table_ref.refs_1_) | copy-start | bytes 6291460
  4.2 32.6 %copy-start.6 = (bf16[64,64]{1,0:T(8,128)(2,1)S(1)}, bf16[64,64]{1,0:T(8,128)(2,1)}, u32[]{:S(2)}) copy-start(bf16[64,64]{1,0:T(8,128)(2,1)} %refs_3_.3) | copy-start | bytes 24580
  36.8 19.9 %copy-start.4 = (bf16[2,256,256]{2,1,0:T(8,128)(2,1)S(1)}, bf16[2,256,256]{2,1,0:T(8,128)(2,1)}, u32[]{:S(2)}) copy-start(bf16[2,256,256]{2,1,0:T(8,128)(2,1)} %constant.16.clone.refs_3_) | copy-start | bytes 786436
  59.4 12.8 %all-to-all-start.3 = ((bf16[32,8,512]{2,1,0:T(8,128)(2,1)}), bf16[32,8,512]{2,1,0:T(8,128)(2,1)S(1)}, u32[]{:S(2)}, u32[]{:S(2)}) async-start(bf16[32,8,512]{2,1,0:T(8,128)(2,1)} %get-tuple-element.33), calls=%async_computation.3 | async-start | bytes 524288 | tf_op jit(solution)/shard_map/all_to_all | solution.py:391
  63.1 5.1 %collective-permute-start = (bf16[2,4,32,128]{3,2,1,0:T(8,128)(2,1)S(1)}, bf16[2,4,32,128]{3,2,1,0:T(8,128)(2,1)S(1)}, u32[]{:S(2)}, u32[]{:S(2)}) collective-permute-start(bf16[2,4,32,128]{3,2,1,0:T(8,128)(2,1)S(1)} %get-tuple-element.36), channel_id=1, source_target_pairs={{0,32},{32,64},{64,96},{96,0},{1,33},{33,65},{65,97},{97,1},{2,34}... | collective-permute-start | bytes 196616 | tf_op jit(solution)/shard_map/ppermute | solution.py:416
  64.5 5.7 %collective-permute-start.1 = (bf16[2,4,32,128]{3,2,1,0:T(8,128)(2,1)S(1)}, bf16[2,4,32,128]{3,2,1,0:T(8,128)(2,1)S(1)}, u32[]{:S(2)}, u32[]{:S(2)}) collective-permute-start(bf16[2,4,32,128]{3,2,1,0:T(8,128)(2,1)S(1)} %get-tuple-element.37), channel_id=1, source_target_pairs={{0,64},{32,96},{64,0},{96,32},{1,65},{33,97},{65,1},{97,33},{2,66}... | collective-permute-start | bytes 196616 | tf_op jit(solution)/shard_map/ppermute | solution.py:416
  67.0 3.4 %collective-permute-start.2 = (bf16[2,4,32,128]{3,2,1,0:T(8,128)(2,1)S(1)}, bf16[2,4,32,128]{3,2,1,0:T(8,128)(2,1)S(1)}, u32[]{:S(2)}, u32[]{:S(2)}) collective-permute-start(bf16[2,4,32,128]{3,2,1,0:T(8,128)(2,1)S(1)} %get-tuple-element.38), channel_id=1, source_target_pairs={{0,96},{32,0},{64,32},{96,64},{1,97},{33,1},{65,33},{97,65},{2,98}... | collective-permute-start | bytes 196616 | tf_op jit(solution)/shard_map/ppermute | solution.py:416

commit v6 on v5

--- a/solution.py
+++ b/solution.py
@@ -313,10 +313,15 @@
     transpose_back(back_ref, turned_ref, 0, False)
     width = mix_ref.shape[0]
     copies = []
-    for i in range(modes_ref.shape[0]):
-        mode_products(shared_refs, modes_ref, i)
-        copies.append(pltpu.make_async_copy(modes_ref.at[i], modes_hbm.at[i], sem_ref.at[1, i]))
-        copies[-1].start()
+
+    def modes(first, last):
+        for i in range(first, last):
+            mode_products(shared_refs, modes_ref, i)
+            copies.append(pltpu.make_async_copy(modes_ref.at[i], modes_hbm.at[i], sem_ref.at[1, i]))
+            copies[-1].start()
+
+    mode_rows = modes_ref.shape[0]
+    modes(0, mode_rows // 2)
     for k, cols in enumerate(tiles(table_ref.shape[1], LOAD_TILE)):
         loads.wait(k)
         for n, at in enumerate(range(0, delta_ref.shape[0], width)):
@@ -331,6 +336,7 @@
                 )
             )
             copies[-1].start()
+    modes(mode_rows // 2, mode_rows)
     for copy in copies:
         copy.wait()
 

time: 78 us -> 78.3 us (level)
  no operation moved by 1% of the time
where the time goes in v6:
time: 78.3 us; the launch traced here: 78 us
  blocking collectives  43.6 us (56%)
  Pallas kernels  20.7 us (26%)
  starting transfers between devices  8.77 us (11%)
  waiting for transfers between devices  4.04 us (5%)
  between operations  0.9 us (1%)
    all_to_all x3, blocking collectives, exchange(): return lax.all_to_all(values, 'space', 0, 0, tiled=True)  43.6 us
    pallas_call x1, Pallas kernels, on_device(): pl.pallas_call(field_kernel, out_shape=[lines_shape, lines_shape, exchang...  7.45 us
    pallas_call x1, Pallas kernels, on_device(): pl.pallas_call(lambda *refs: grad_kernel(*refs, samples=samples), out_sha...  5.69 us
    ppermute x3, starting transfers between devices, share(): lax.ppermute(blocks[k], 'dp', [(a, (a + k) % samples) for a in range(samp...  5.06 us
    pallas_call x2, Pallas kernels, mix(): pl.pallas_call(lambda *refs: modes_kernel(*refs, adjoint=adjoint, samples...  4.06 us
    all_to_all x1, starting transfers between devices, exchange(): return lax.all_to_all(values, 'space', 0, 0, tiled=True)  3.71 us
    pallas_call x1, Pallas kernels, on_device(): pl.pallas_call(columns_kernel, out_shape=[exchange_shape, jax.ShapeDtypeS...  3.52 us
    ppermute x3, waiting for transfers between devices, share(): lax.ppermute(blocks[k], 'dp', [(a, (a + k) % samples) for a in range(samp...  2.27 us
  transfers between devices with their start and end apart: 4, of which 3 were waited for; matrix products, arithmetic and copies ran while one was open for 0% of the time, Pallas kernels for 0%

profile of v6, /device:TPU:1, one launch (start us, length us, event | category | flops | bytes accessed | tf_op | source)
XLA Modules:
  0.0 78.0 jit_solution(599087941526382833)
XLA Ops:
  0.6 0.0 copy-start
  0.6 0.0 copy-start.3
  0.7 0.0 copy-start.5
  0.7 0.0 copy-start.2
  0.7 3.5 %columns.1 = (bf16[32,8,512]{2,1,0:T(8,128)(2,1)S(1)}, bf16[512,4096]{1,0:T(8,128)(2,1)S(1)}) custom-call(bf16[256,4096]{1,0:T(8,128)(2,1)} %constant.14.clone.table_hbm.table_ref.refs_1_, bf16[512,4096]{1,0:T(8,128)(2,1)} %bitcast.7, bf16[512,4096]{1,0:T(8,128)(2,1)} %bitcast.5, bf16[4,64,64,128]{3,2,1,0:T(8,128)(2,1)} %refs_2_.3), custom_call_target="tpu_custom_call" | custom-call | bytes 16777216 | tf_op jit(solution)/shard_map/columns/pallas_call | solution.py:428
  4.2 0.0 copy-start.1
  4.2 0.0 copy-start.6
  4.2 18.7 %all_to_all.20.refs_1_ = bf16[32,8,512]{2,1,0:T(8,128)(2,1)S(1)} all-to-all(bf16[32,8,512]{2,1,0:T(8,128)(2,1)S(1)} %get-tuple-element.24), channel_id=1, replica_groups=mesh['dp'=4,'space'=32] {'space'}, dimensions={0} | all-to-all | bytes 524288 | tf_op jit(solution)/shard_map/all_to_all | solution.py:397
  22.9 0.0 copy-done.5
  22.9 1.4 %mix_modes.1 = (bf16[32,8,512]{2,1,0:T(8,128)(2,1)S(1)}, bf16[4,32,128]{2,1,0:T(8,128)(2,1)S(1)}, bf16[4,32,128]{2,1,0:T(8,128)(2,1)S(1)}, bf16[4,32,128]{2,1,0:T(8,128)(2,1)S(1)}, bf16[4,32,128]{2,1,0:T(8,128)(2,1)S(1)}) custom-call(s32[1]{0:T(128)} %bitcast.2.refs_0_, bf16[32,8,512]{2,1,0:T(8,128)(2,1)S(1)} %all_to_all.20.refs_1_, ...), custom_call_target="tpu_custom_call" | custom-call | bytes 16777216 | tf_op jit(solution)/shard_map/mix_modes/pallas_call | solution.py:403
  24.3 12.5 %all_to_all.21.back_ref = bf16[32,8,512]{2,1,0:T(8,128)(2,1)S(1)} all-to-all(bf16[32,8,512]{2,1,0:T(8,128)(2,1)S(1)} %get-tuple-element.25), channel_id=1, replica_groups=mesh['dp'=4,'space'=32] {'space'}, dimensions={0} | all-to-all | bytes 524288 | tf_op jit(solution)/shard_map/all_to_all | solution.py:397
  36.8 0.0 copy-start.4
  36.8 7.5 %field_step.1 = (bf16[512,4096]{1,0:T(8,128)(2,1)}, bf16[512,4096]{1,0:T(8,128)(2,1)}, bf16[32,8,512]{2,1,0:T(8,128)(2,1)S(1)}) custom-call(bf16[32,8,512]{2,1,0:T(8,128)(2,1)S(1)} %all_to_all.21.back_ref, bf16[256,4096]{1,0:T(8,128)(2,1)S(1)} %copy-done.1, bf16[512,4096]{1,0:T(8,128)(2,1)S(1)} %get-tuple-element.26.fields_ref, ...), custom_call_target="tpu_custom_call" | custom-call | bytes 25165824 | tf_op jit(solution)/shard_map/field_step/pallas_call | solution.py:445
  44.2 12.4 %all_to_all.22.refs_1_ = bf16[32,8,512]{2,1,0:T(8,128)(2,1)S(1)} all-to-all(bf16[32,8,512]{2,1,0:T(8,128)(2,1)S(1)} %get-tuple-element.28), channel_id=1, replica_groups=mesh['dp'=4,'space'=32] {'space'}, dimensions={0} | all-to-all | bytes 524288 | tf_op jit(solution)/shard_map/all_to_all | solution.py:397
  56.7 2.7 %adjoint_modes.1 = (bf16[32,8,512]{2,1,0:T(8,128)(2,1)}, bf16[2,4,32,128]{3,2,1,0:T(8,128)(2,1)S(1)}, bf16[2,4,32,128]{3,2,1,0:T(8,128)(2,1)S(1)}, bf16[2,4,32,1...) custom-call(s32[1]{0:T(128)} %bitcast.2.refs_0_, bf16[32,8,512]{2,1,0:T(8,128)(2,1)S(1)} %all_to_all.22.refs_1_, ...), custom_call_target="tpu_custom_call" | custom-call | bytes 16777216 | tf_op jit(solution)/shard_map/adjoint_modes/pallas_call | solution.py:403
  59.4 3.7 %all-to-all-start.3 = ((bf16[32,8,512]{2,1,0:T(8,128)(2,1)}), bf16[32,8,512]{2,1,0:T(8,128)(2,1)S(1)}, u32[]{:S(2)}, u32[]{:S(2)}) async-start(bf16[32,8,512]{2,1,0:T(8,128)(2,1)} %get-tuple-element.33), calls=%async_computation.3 | async-start | bytes 524288 | tf_op jit(solution)/shard_map/all_to_all | solution.py:397
  63.1 1.5 %collective-permute-start = (bf16[2,4,32,128]{3,2,1,0:T(8,128)(2,1)S(1)}, bf16[2,4,32,128]{3,2,1,0:T(8,128)(2,1)S(1)}, u32[]{:S(2)}, u32[]{:S(2)}) collective-permute-start(bf16[2,4,32,128]{3,2,1,0:T(8,128)(2,1)S(1)} %get-tuple-element.36), channel_id=1, source_target_pairs={{0,32},{32,64},{64,96},{96,0},{1,33},{33,65},{65,97},{97,1},{2,34}... | collective-permute-start | bytes 196616 | tf_op jit(solution)/shard_map/ppermute | solution.py:422
  64.5 2.5 %collective-permute-start.1 = (bf16[2,4,32,128]{3,2,1,0:T(8,128)(2,1)S(1)}, bf16[2,4,32,128]{3,2,1,0:T(8,128)(2,1)S(1)}, u32[]{:S(2)}, u32[]{:S(2)}) collective-permute-start(bf16[2,4,32,128]{3,2,1,0:T(8,128)(2,1)S(1)} %get-tuple-element.37), channel_id=1, source_target_pairs={{0,64},{32,96},{64,0},{96,32},{1,65},{33,97},{65,1},{97,33},{2,66}... | collective-permute-start | bytes 196616 | tf_op jit(solution)/shard_map/ppermute | solution.py:422
  67.0 1.1 %collective-permute-start.2 = (bf16[2,4,32,128]{3,2,1,0:T(8,128)(2,1)S(1)}, bf16[2,4,32,128]{3,2,1,0:T(8,128)(2,1)S(1)}, u32[]{:S(2)}, u32[]{:S(2)}) collective-permute-start(bf16[2,4,32,128]{3,2,1,0:T(8,128)(2,1)S(1)} %get-tuple-element.38), channel_id=1, source_target_pairs={{0,96},{32,0},{64,32},{96,64},{1,97},{33,1},{65,33},{97,65},{2,98}... | collective-permute-start | bytes 196616 | tf_op jit(solution)/shard_map/ppermute | solution.py:422
  68.1 0.0 collective-permute-done.refs_5_
  68.1 2.1 %collective-permute-done.1.refs_6_ = bf16[2,4,32,128]{3,2,1,0:T(8,128)(2,1)S(1)} collective-permute-done((bf16[2,4,32,128]{3,2,1,0:T(8,128)(2,1)S(1)}, bf16[2,4,32,128]{3,2,1,0:T(8,128)(2,1)S(1)}, u32[]{:S(2)}, u32[]{:S(2)}) %collective-permute-start.1) | collective-permute-done | bytes 65568 | tf_op jit(solution)/shard_map/ppermute | solution.py:422
  70.3 0.1 collective-permute-done.2.refs_7_
  70.4 1.8 %all-to-all-done.3.refs_0_ = bf16[32,8,512]{2,1,0:T(8,128)(2,1)S(1)} async-done(((bf16[32,8,512]{2,1,0:T(8,128)(2,1)}), bf16[32,8,512]{2,1,0:T(8,128)(2,1)S(1)}, u32[]{:S(2)}, u32[]{:S(2)}) %all-to-all-start.3) | async-done | bytes 262176 | tf_op jit(solution)/shard_map/all_to_all | solution.py:397
  72.2 5.7 %gradients.1 = (bf16[512,4096]{1,0:T(8,128)(2,1)}, f32[4,16,64,128]{3,2,1,0:T(8,128)}) custom-call(bf16[32,8,512]{2,1,0:T(8,128)(2,1)S(1)} %all-to-all-done.3.refs_0_, bf16[256,4096]{1,0:T(8,128)(2,1)S(1)} %copy-done.1, bf16[512,4096]{1,0:T(8,128)(2,1)} %get-tuple-element.34.refs_2_, bf16[64,64]{1,0:T(8,128)(2,1)S(1)} %copy-done.6, ...), custom_call_target="tpu_custom_call" | custom-call | bytes 16777216 | tf_op jit(solution)/shard_map/gradients/pallas_call | solution.py:466
  (6 shorter events, 0.0 us)
Async XLA Ops:
  0.6 22.3 %copy-start = (bf16[4,64,64,128]{3,2,1,0:T(8,128)(2,1)S(1)}, bf16[4,64,64,128]{3,2,1,0:T(8,128)(2,1)}, u32[]{:S(2)}) copy-start(bf16[4,64,64,128]{3,2,1,0:T(8,128)(2,1)} %refs_2_.3) | copy-start | bytes 12582916
  0.6 22.2 %copy-start.3 = (bf16[2,256,128]{2,1,0:T(8,128)(2,1)S(1)}, bf16[2,256,128]{2,1,0:T(8,128)(2,1)}, u32[]{:S(2)}) copy-start(bf16[2,256,128]{2,1,0:T(8,128)(2,1)} %constant.17.clone.refs_4_) | copy-start | bytes 393220
  0.7 22.2 %copy-start.5 = (bf16[2,256,256]{2,1,0:T(8,128)(2,1)S(1)}, bf16[2,256,256]{2,1,0:T(8,128)(2,1)}, u32[]{:S(2)}) copy-start(bf16[2,256,256]{2,1,0:T(8,128)(2,1)} %constant.15.clone.refs_3_) | copy-start | bytes 786436
  0.7 36.1 %copy-start.2 = (bf16[1,8,64,4096]{3,2,1,0:T(8,128)(2,1)S(1)}, bf16[1,8,64,4096]{3,2,1,0:T(8,128)(2,1)}, u32[]{:S(2)}) copy-start(bf16[1,8,64,4096]{3,2,1,0:T(8,128)(2,1)} %param.9) | copy-start | bytes 12582916
  4.2 32.6 %copy-start.1 = (bf16[256,4096]{1,0:T(8,128)(2,1)S(1)}, bf16[256,4096]{1,0:T(8,128)(2,1)}, u32[]{:S(2)}) copy-start(bf16[256,4096]{1,0:T(8,128)(2,1)} %constant.14.clone.table_hbm.table_ref.refs_1_) | copy-start | bytes 6291460
  4.2 32.6 %copy-start.6 = (bf16[64,64]{1,0:T(8,128)(2,1)S(1)}, bf16[64,64]{1,0:T(8,128)(2,1)}, u32[]{:S(2)}) copy-start(bf16[64,64]{1,0:T(8,128)(2,1)} %refs_3_.3) | copy-start | bytes 24580
  36.8 19.9 %copy-start.4 = (bf16[2,256,256]{2,1,0:T(8,128)(2,1)S(1)}, bf16[2,256,256]{2,1,0:T(8,128)(2,1)}, u32[]{:S(2)}) copy-start(bf16[2,256,256]{2,1,0:T(8,128)(2,1)} %constant.16.clone.refs_3_) | copy-start | bytes 786436
  59.4 12.8 %all-to-all-start.3 = ((bf16[32,8,512]{2,1,0:T(8,128)(2,1)}), bf16[32,8,512]{2,1,0:T(8,128)(2,1)S(1)}, u32[]{:S(2)}, u32[]{:S(2)}) async-start(bf16[32,8,512]{2,1,0:T(8,128)(2,1)} %get-tuple-element.33), calls=%async_computation.3 | async-start | bytes 524288 | tf_op jit(solution)/shard_map/all_to_all | solution.py:397
  63.1 5.1 %collective-permute-start = (bf16[2,4,32,128]{3,2,1,0:T(8,128)(2,1)S(1)}, bf16[2,4,32,128]{3,2,1,0:T(8,128)(2,1)S(1)}, u32[]{:S(2)}, u32[]{:S(2)}) collective-permute-start(bf16[2,4,32,128]{3,2,1,0:T(8,128)(2,1)S(1)} %get-tuple-element.36), channel_id=1, source_target_pairs={{0,32},{32,64},{64,96},{96,0},{1,33},{33,65},{65,97},{97,1},{2,34}... | collective-permute-start | bytes 196616 | tf_op jit(solution)/shard_map/ppermute | solution.py:422
  64.5 5.7 %collective-permute-start.1 = (bf16[2,4,32,128]{3,2,1,0:T(8,128)(2,1)S(1)}, bf16[2,4,32,128]{3,2,1,0:T(8,128)(2,1)S(1)}, u32[]{:S(2)}, u32[]{:S(2)}) collective-permute-start(bf16[2,4,32,128]{3,2,1,0:T(8,128)(2,1)S(1)} %get-tuple-element.37), channel_id=1, source_target_pairs={{0,64},{32,96},{64,0},{96,32},{1,65},{33,97},{65,1},{97,33},{2,66}... | collective-permute-start | bytes 196616 | tf_op jit(solution)/shard_map/ppermute | solution.py:422
  67.0 3.4 %collective-permute-start.2 = (bf16[2,4,32,128]{3,2,1,0:T(8,128)(2,1)S(1)}, bf16[2,4,32,128]{3,2,1,0:T(8,128)(2,1)S(1)}, u32[]{:S(2)}, u32[]{:S(2)}) collective-permute-start(bf16[2,4,32,128]{3,2,1,0:T(8,128)(2,1)S(1)} %get-tuple-element.38), channel_id=1, source_target_pairs={{0,96},{32,0},{64,32},{96,64},{1,97},{33,1},{65,33},{97,65},{2,98}... | collective-permute-start | bytes 196616 | tf_op jit(solution)/shard_map/ppermute | solution.py:422
